TPU v7x, 128 devices: a whole 4x4x4 slice. The times are simulated.
128 devices in a mesh: bx: 32 (over x, z, core), by: 2 (over y_hi), col: 2 (over y_lo).
Axes of the slice: x: 4, y: 4 (y_hi: 2, y_lo: 2; y = y_hi * 2 + y_lo), z: 4, core: 2. Of those that a mesh axis runs over, the one named last changes fastest.
Arguments:
- multipoles: bfloat16 [2, 152, 32, 1024], P(None, 'col', 'bx', 'by'), may hold values from -6 to 6
- kernel: bfloat16 [2, 32, 32, 17, 152, 152], P(None, 'bx', 'by', None, 'col'), may hold values from -0.5 to 0.5
Outputs:
- locals_out: float32 [2, 152, 32, 1024], P(None, 'col', 'bx', 'by')
All inputs are finite; a program needn't handle non-finite values.
Results may differ from a plain program's by a relative error of at most 0.0029.
Values may be sent and summed in bfloat16 or wider, within the bound.
No kernel may reach another device: no remote copies, remote signals or barrier semaphores. Data moves between devices by JAX's collectives and lax.ppermute only.
A program may use at most 128 MiB of HBM per device.

v0:
```python
import math

import jax
import jax.numpy as jnp
from jax import lax
from jax.sharding import PartitionSpec as P

NB = 32
KZ = 17


precise = lax.Precision.HIGHEST


def angle_table(count_in, count_out):
    left_index = jnp.arange(count_in, dtype=jnp.int32)[:, None]
    second = jnp.arange(count_out, dtype=jnp.int32)[None, :]
    phases = (left_index * second % count_in).astype(jnp.float32) * (2.0 * math.pi / count_in)
    return (jnp.cos(phases), jnp.sin(phases))


def contract(pattern, values, table):
    return jnp.einsum(pattern, values, table, precision=precise)


def to_planes(spatial):
    return lax.all_to_all(
        lax.all_to_all(spatial, "bx", split_axis=4, concat_axis=2, tiled=True),
        "by",
        split_axis=0,
        concat_axis=3,
        tiled=True,
    )


def to_columns(waves):
    return lax.all_to_all(
        lax.all_to_all(waves, "bx", split_axis=3, concat_axis=5, tiled=True),
        "by",
        split_axis=4,
        concat_axis=1,
        tiled=True,
    )


def back_planes(columns):
    return lax.all_to_all(
        lax.all_to_all(columns, "bx", split_axis=5, concat_axis=3, tiled=True),
        "by",
        split_axis=1,
        concat_axis=4,
        tiled=True,
    )


def back_boxes(planes):
    return lax.all_to_all(
        lax.all_to_all(planes, "bx", split_axis=2, concat_axis=4, tiled=True),
        "by",
        split_axis=3,
        concat_axis=0,
        tiled=True,
    )


def kernel_terms(kernel_part, panel):
    pattern = "abkij,rjabk->riabk"
    real_part = jnp.einsum(
        pattern, kernel_part[0], panel[0], preferred_element_type=jnp.float32
    ) - jnp.einsum(pattern, kernel_part[1], panel[1], preferred_element_type=jnp.float32)
    imag_part = jnp.einsum(
        pattern, kernel_part[0], panel[1], preferred_element_type=jnp.float32
    ) + jnp.einsum(pattern, kernel_part[1], panel[0], preferred_element_type=jnp.float32)
    return (real_part, imag_part)


def apply_kernel(spectrum, kernel):
    panels = lax.all_gather(spectrum, "col", axis=2, tiled=True)
    return kernel_terms(kernel, panels)


def on_device(multipoles, kernel):
    rhs_count, coeffs, x_local, plane_cells = multipoles.shape
    grid_side = NB
    cos_grid, sin_grid = angle_table(grid_side, grid_side)
    cos_half, sin_half = angle_table(grid_side, KZ)
    spatial_raw = multipoles.reshape(
        rhs_count, coeffs, x_local, plane_cells // grid_side, grid_side
    )
    along_x = "rcxyz,xk->rckyz"
    along_y = "rckyz,yl->rcklz"
    planes = to_planes(spatial_raw).astype(jnp.float32)
    first_re = contract(along_x, planes, cos_grid)
    first_im = -contract(along_x, planes, sin_grid)
    wave_re = contract(along_y, first_re, cos_grid) + contract(along_y, first_im, sin_grid)
    wave_im = contract(along_y, first_im, cos_grid) - contract(along_y, first_re, sin_grid)
    columns = to_columns(jnp.stack([wave_re, wave_im]))
    along_z = "rcabz,zk->rcabk"
    spec_re = contract(along_z, columns[0], cos_half) + contract(along_z, columns[1], sin_half)
    spec_im = contract(along_z, columns[1], cos_half) - contract(along_z, columns[0], sin_half)
    spectrum = jnp.stack([spec_re, spec_im]).astype(jnp.bfloat16)
    local_re, local_im = apply_kernel(spectrum, kernel)
    freq_index = jnp.arange(KZ, dtype=jnp.int32)
    weights = jnp.where((freq_index == 0) | (freq_index == grid_side // 2), 1.0, 2.0).astype(
        jnp.float32
    )
    cos_back = cos_half * weights[None, :]
    sin_back = sin_half * weights[None, :]
    from_z = "rcabk,zk->rcabz"
    back_re = contract(from_z, local_re, cos_back) - contract(from_z, local_im, sin_back)
    back_im = contract(from_z, local_re, sin_back) + contract(from_z, local_im, cos_back)
    planes_back = back_planes(jnp.stack([back_re, back_im]))
    turn_re = contract(along_x, planes_back[0], cos_grid) - contract(
        along_x, planes_back[1], sin_grid
    )
    turn_im = contract(along_x, planes_back[0], sin_grid) + contract(
        along_x, planes_back[1], cos_grid
    )
    spatial_out = (contract(along_y, turn_re, cos_grid) - contract(along_y, turn_im, sin_grid)) * (
        1.0 / float(grid_side**3)
    )
    result = back_boxes(spatial_out)
    return result.reshape(rhs_count, coeffs, x_local, plane_cells)


def solution(mesh):
    placed = (P(None, "col", "bx", "by"), P(None, "bx", "by", None, "col", None))
    return jax.shard_map(
        on_device, mesh=mesh, in_specs=placed, out_specs=P(None, "col", "bx", "by"), check_vma=False
    )
```

profile of v0, /device:TPU:1, one launch (start us, length us, event | category | flops | bytes accessed | tf_op | source)
XLA Modules:
  0.0 250.1 jit_solution(13036597349925570126)
XLA Ops:
  0.0 1.1 copy.42
  1.1 0.1 copy.43
  1.2 18.2 %all_to_all.132 = bf16[2,76,1,16,32]{1,3,0,2,4:T(8,128)(2,1)S(1)} all-to-all(bf16[2,76,1,16,32]{1,3,0,2,4:T(8,128)(2,1)S(1)} %copy.43), channel_id=1, replica_groups=mesh['bx'=32,'by'=2,'col'=2] {'bx'}, dimensions={4} | all-to-all | bytes 311296 | tf_op jit(solution)/shard_map/all_to_all | solution.py:28
  19.4 0.1 copy.44
  19.5 10.3 %all_to_all.133 = bf16[2,76,32,16,1]{1,2,3,4,0:T(8,128)(2,1)S(1)} all-to-all(bf16[2,76,32,16,1]{1,2,3,4,0:T(8,128)(2,1)S(1)} %copy.44), channel_id=1, replica_groups=mesh['bx'=32,'by'=2,'col'=2] {'by'}, dimensions={0} | all-to-all | bytes 311296 | tf_op jit(solution)/shard_map/all_to_all | solution.py:27
  29.8 0.4 fusion.8
  30.2 0.4 convolution_bitcast_fusion
  30.7 0.9 fusion.42
  31.6 0.9 fusion.38
  32.5 0.9 fusion.16
  33.4 0.9 fusion.15
  34.3 0.1 pad_maximum_fusion
  34.4 0.1 copy.49
  34.5 21.3 %all_to_all.134 = f32[2,1,76,32,32,1]{2,4,5,1,0,3:T(8,128)S(1)} all-to-all(f32[2,1,76,32,32,1]{2,4,5,1,0,3:T(8,128)S(1)} %copy.49), channel_id=1, replica_groups=mesh['bx'=32,'by'=2,'col'=2] {'bx'}, dimensions={3} | all-to-all | bytes 1245184 | tf_op jit(solution)/shard_map/all_to_all | solution.py:38
  55.8 1.6 copy.50
  57.4 3.6 %all-to-all-start.3 = ((f32[2,1,76,1,32,32]{2,5,0,3,1,4:T(8,128)}), f32[2,1,76,1,32,32]{2,5,0,3,1,4:T(8,128)S(1)}, u32[]{:S(2)}, u32[]{:S(2)}) async-start(f32[2,1,76,1,32,32]{2,5,0,3,1,4:T(8,128)} %copy.50), calls=%async_computation.3 | async-start | bytes 2097152 | tf_op jit(solution)/shard_map/all_to_all | solution.py:37
  61.0 15.2 %fusion.200 = (bf16[1,1,16,17,76,152]{5,2,4,3,1,0:T(8,128)(2,1)}, bf16[1,1,16,17,76,152]{5,2,4,3,1,0:T(8,128)(2,1)}) fusion(bf16[2,1,16,17,76,152]{5,2,4,3,1,0:T(8,128)(2,1)} %param.3), kind=kLoop, calls=%fused_computation.195 | loop fusion | bytes 25137152 | tf_op jit(solution)/shard_map/slice | solution.py:69
  76.2 18.9 %copy.73 = bf16[1,1,16,17,76,152]{4,5,3,2,1,0:T(8,128)(2,1)} copy(bf16[1,1,16,17,76,152]{5,2,4,3,1,0:T(8,128)(2,1)} %get-tuple-element.5) | data formatting | bytes 12568576
  95.1 18.8 %copy.75 = bf16[1,1,16,17,76,152]{4,5,3,2,1,0:T(8,128)(2,1)} copy(bf16[1,1,16,17,76,152]{5,2,4,3,1,0:T(8,128)(2,1)} %get-tuple-element.6) | data formatting | bytes 12568576
  113.9 0.0 all-to-all-done.3
  114.0 0.1 copy.51
  114.0 0.5 fusion.37
  114.6 0.5 fusion.36
  115.1 0.6 fusion.19
  115.7 0.6 fusion.20
  116.3 0.1 pad_maximum_fusion.2
  116.4 2.2 copy.52
  118.6 29.5 %all_gather.3 = bf16[2,2,152,1,16,17]{5,4,3,1,0,2:T(8,128)(2,1)S(1)} all-gather(bf16[2,2,76,1,16,17]{5,4,3,1,0,2:T(8,128)(2,1)S(1)} %copy.52), channel_id=1, replica_groups=mesh['bx'=32,'by'=2,'col'=2] {'col'}, dimensions={2}, use_global_device_ids=true | all-gather | bytes 496128 | tf_op jit(solution)/shard_map/all_gather | solution.py:78
  148.1 0.4 fusion.201
  148.5 1.4 copy.72
  149.9 1.6 copy.74
  151.5 0.0 slice-start
  151.5 0.0 slice-start.1
  151.5 7.1 %fusion = f32[16,17,2,76]{3,2,1,0:T(2,128)S(1)} fusion(bf16[1,1,16,17,76,152]{4,5,3,2,1,0:T(8,128)(2,1)} %copy.75, bf16[1,2,152,1,16,17]{2,1,5,4,3,0:T(2,128)(2,1)S(1)} %copy.72), kind=kOutput, calls=%fused_computation | convolution fusion | flops 12568576 | bytes 6615040 | tf_op jit(solution)/shard_map/abkij,rjabk->riabk/dot_general | solution.py:73
  158.6 0.0 slice-start.2
  158.6 7.1 %fusion.2 = f32[16,17,2,76]{3,2,1,0:T(2,128)S(1)} fusion(bf16[1,1,16,17,76,152]{4,5,3,2,1,0:T(8,128)(2,1)} %copy.75, bf16[1,2,152,1,16,17]{2,1,5,4,3,0:T(2,128)(2,1)S(1)} %copy.74), kind=kOutput, calls=%fused_computation.2 | convolution fusion | flops 12568576 | bytes 6615040 | tf_op jit(solution)/shard_map/abkij,rjabk->riabk/dot_general | solution.py:70
  165.6 0.0 slice-done
  165.7 0.0 slice-done.1
  165.7 0.0 slice-done.2
  165.7 3.0 %fusion.24 = f32[2,76,16,17]{1,0,3,2:T(2,128)S(1)} fusion(f32[16,17,2,76]{3,2,1,0:T(2,128)S(1)} %fusion.2, bf16[1,1,16,17,76,152]{4,5,3,2,1,0:T(8,128)(2,1)S(1)} %bitcast.198, bf16[1,2,152,1,16,17]{2,1,5,4,3,0:T(2,128)(2,1)S(1)} %copy.72), kind=kOutput, calls=%fused_computation.33 | convolution fusion | flops 12609920 | bytes 6780416 | tf_op jit(solution)/shard_map/abkij,rjabk->riabk/dot_general | solution.py:68
  168.7 0.7 fusion.46
  169.4 0.7 fusion.48
  170.1 3.0 %fusion.30 = f32[2,76,16,17]{1,0,3,2:T(2,128)S(1)} fusion(f32[16,17,2,76]{3,2,1,0:T(2,128)S(1)} %fusion, bf16[1,1,16,17,76,152]{4,5,3,2,1,0:T(8,128)(2,1)S(1)} %bitcast.198, bf16[1,2,152,1,16,17]{2,1,5,4,3,0:T(2,128)(2,1)S(1)} %copy.74), kind=kOutput, calls=%fused_computation.35 | convolution fusion | flops 12609920 | bytes 6780416 | tf_op jit(solution)/shard_map/abkij,rjabk->riabk/dot_general | solution.py:71
  173.0 0.7 fusion.13
  173.7 0.7 fusion.14
  174.4 0.1 pad_maximum_fusion.1
  174.5 0.8 copy.61
  175.4 21.2 %all_to_all.135 = f32[2,2,76,1,16,32]{2,4,1,3,0,5:T(8,128)S(1)} all-to-all(f32[2,2,76,1,16,32]{2,4,1,3,0,5:T(8,128)S(1)} %copy.61), channel_id=1, replica_groups=mesh['bx'=32,'by'=2,'col'=2] {'bx'}, dimensions={5} | all-to-all | bytes 1245184 | tf_op jit(solution)/shard_map/all_to_all | solution.py:48
  196.6 0.6 copy.62
  197.2 18.8 %all_to_all.136 = f32[2,2,76,32,16,1]{2,3,4,0,5,1:T(8,128)S(1)} all-to-all(f32[2,2,76,32,16,1]{2,3,4,0,5,1:T(8,128)S(1)} %copy.62), channel_id=1, replica_groups=mesh['bx'=32,'by'=2,'col'=2] {'by'}, dimensions={1} | all-to-all | bytes 1245184 | tf_op jit(solution)/shard_map/all_to_all | solution.py:47
  216.0 0.1 fusion.202
  216.0 0.7 fusion.58
  216.7 0.7 fusion.66
  217.4 0.7 fusion.12
  218.0 0.7 fusion.11
  218.7 0.9 fusion.34
  219.6 0.9 fusion.10
  220.5 16.1 %all_to_all.137 = f32[1,76,32,32,1]{1,3,4,0,2:T(8,128)S(1)} all-to-all(f32[1,76,32,32,1]{1,3,4,0,2:T(8,128)S(1)} %fusion.10), channel_id=1, replica_groups=mesh['bx'=32,'by'=2,'col'=2] {'bx'}, dimensions={2} | all-to-all | bytes 622592 | tf_op jit(solution)/shard_map/all_to_all | solution.py:58
  236.6 0.3 copy.66
  236.9 12.3 %all_to_all.138 = f32[1,76,1,32,32]{1,4,2,0,3:T(8,128)S(1)} all-to-all(f32[1,76,1,32,32]{1,4,2,0,3:T(8,128)S(1)} %copy.66), channel_id=1, replica_groups=mesh['bx'=32,'by'=2,'col'=2] {'by'}, dimensions={3} | all-to-all | bytes 622592 | tf_op jit(solution)/shard_map/all_to_all | solution.py:57
  249.2 0.9 copy.67
  (2 shorter events, 0.0 us)
Async XLA Ops:
  57.4 56.5 %all-to-all-start.3 = ((f32[2,1,76,1,32,32]{2,5,0,3,1,4:T(8,128)}), f32[2,1,76,1,32,32]{2,5,0,3,1,4:T(8,128)S(1)}, u32[]{:S(2)}, u32[]{:S(2)}) async-start(f32[2,1,76,1,32,32]{2,5,0,3,1,4:T(8,128)} %copy.50), calls=%async_computation.3 | async-start | bytes 2097152 | tf_op jit(solution)/shard_map/all_to_all | solution.py:37
  151.5 14.2 %slice-start = ((s8[10584064]{0:T(1024)(128)(4,1)}), s8[4194304]{0:T(1024)(128)(4,1)S(1)}, s32[]{:S(2)}) async-start(s8[10584064]{0:T(1024)(128)(4,1)} %bitcast.197), calls=%async_computation.8 | async-start | bytes 8388608
  151.5 14.2 %slice-start.1 = ((s8[10584064]{0:T(1024)(128)(4,1)}), s8[4194304]{0:T(1024)(128)(4,1)S(1)}, s32[]{:S(2)}) async-start(s8[10584064]{0:T(1024)(128)(4,1)} %bitcast.197), calls=%async_computation.9 | async-start | bytes 8388608
  158.6 7.1 %slice-start.2 = ((s8[10584064]{0:T(1024)(128)(4,1)}), s8[2195456]{0:T(1024)(128)(4,1)S(1)}, s32[]{:S(2)}) async-start(s8[10584064]{0:T(1024)(128)(4,1)} %bitcast.197), calls=%async_computation.10 | async-start | bytes 4390912
where the time goes:
time: 251 us; the launch traced here: 250 us
  blocking collectives  148 us (59%)
  local copies, waits for them, and re-layouts  64.4 us (26%)
  matrix products  33.9 us (14%)
  starting transfers between devices  3.58 us (1%)
    unnamed x11, local copies, waits for them, and re-layouts  41.8 us
    all_gather x1, blocking collectives, apply_kernel(): panels = lax.all_gather(spectrum, 'col', axis=2, tiled=True)  29.5 us
    all_to_all x1, blocking collectives, to_columns(): lax.all_to_all(waves, 'bx', split_axis=3, concat_axis=5, tiled=True)  21.3 us
    all_to_all x1, blocking collectives, back_planes(): lax.all_to_all(columns, 'bx', split_axis=5, concat_axis=3, tiled=True)  21.2 us
    all_to_all x1, blocking collectives, back_planes(): lax.all_to_all(lax.all_to_all(columns, 'bx', split_axis=5, concat_axis=3,...  18.8 us
    all_to_all x1, blocking collectives, to_planes(): lax.all_to_all(spatial, 'bx', split_axis=4, concat_axis=2, tiled=True)  18.2 us
    all_to_all x1, blocking collectives, back_boxes(): lax.all_to_all(planes, 'bx', split_axis=2, concat_axis=4, tiled=True)  16.1 us
    slice x1, local copies, waits for them, and re-layouts, kernel_terms(): kernel_part[0]  15.2 us
  transfers between devices with their start and end apart: 1, of which 0 were waited for; matrix products, arithmetic and copies ran while one was open for 21% of the time, Pallas kernels for 0%

commit v1 on v0

v1 whole, which is shorter than its diff:
```python
import functools
import math

import jax
import jax.numpy as jnp
import numpy as np
from jax import lax
from jax.experimental import pallas as pl
from jax.experimental.pallas import tpu as pltpu
from jax.sharding import PartitionSpec as P

NB = 32
KZ = 17
RHS = 2
HALF = 38
SPARE = 19
F32 = jnp.float32
BF16 = jnp.bfloat16


def to_bf16(values):
    return np.asarray(values, np.float32).astype(jnp.bfloat16)


def table_scale():
    level = np.cos(2 * np.pi * np.arange(8) / 32)
    weight = np.array([2.0] + [4.0] * 7)
    scales = np.linspace(1.0, 2.0, 20001)[:-1]
    scaled = scales[:, None] * level[None, :]
    error = to_bf16(scaled).astype(np.float64) / scales[:, None] - level[None, :]
    return float(scales[np.argmin((weight * error**2).sum(1))])


SCALE = table_scale()


def split(table):
    high = to_bf16(SCALE * table)
    return high, to_bf16(SCALE * table - high.astype(np.float64))


def tables_z():
    kz = np.arange(KZ)[:, None]
    z = np.arange(NB)[None, :]
    angle = 2 * np.pi * ((kz * z) % NB) / NB
    eye = np.eye(16)
    cos = np.einsum("kz,ab->kabz", np.cos(angle), eye).reshape(KZ * 16, 16 * NB)
    sin = np.einsum("kz,ab->kabz", -np.sin(angle), eye).reshape(KZ * 16, 16 * NB)
    return np.stack(split(cos)), np.stack(split(sin[:256]))


def table_line():
    k = np.arange(NB)
    angle = 2 * np.pi * ((k[:, None] * k[None, :]) % NB) / NB
    high, low = split(np.concatenate([np.cos(angle), np.sin(angle)]))
    return np.concatenate([high, low, high], 1)


def select_in():
    table = np.zeros((4, 128, 512), np.float32)
    c = np.arange(HALF)
    for half in range(2):
        for column in range(2):
            target = column * 76 + half * HALF + c
            table[half * 2 + column, c, target] = 1
            table[half * 2 + column, 64 + c, 256 + target] = 1
    return to_bf16(table)


def select_out():
    table = np.zeros((2, 256, 128), np.float32)
    c = np.arange(HALF)
    for half in range(2):
        table[half, half * HALF + c, c] = 1
        table[half, 128 + half * HALF + c, 64 + c] = 1
    return to_bf16(table)


def lane_index(rows):
    return lax.broadcasted_iota(jnp.int32, (rows, 128), 1)


def lanes_between(rows, low, high):
    lane = lane_index(rows) % 64
    return (lane >= low) & (lane < high)


def dot_nt(left, right):
    return lax.dot_general(left, right, (((1,), (1,)), ((), ())), preferred_element_type=F32)


def dot_tn(left, right):
    return lax.dot_general(left, right, (((0,), (0,)), ((), ())), preferred_element_type=F32)


def dot(left, right):
    return jnp.dot(left, right, preferred_element_type=F32)


def spread_last(last, rows):
    spare = lanes_between(rows, HALF, HALF + SPARE)
    first = jnp.where(spare, pltpu.roll(last, HALF, 1), 0.0)
    second = jnp.where(spare, pltpu.roll(last, HALF - SPARE, 1), 0.0)
    return first, second


def gather_last(first, second, rows):
    first = jnp.where(lanes_between(rows, 0, SPARE), pltpu.roll(first, 128 - HALF, 1), 0.0)
    second = jnp.where(
        lanes_between(rows, SPARE, HALF), pltpu.roll(second, 128 - HALF + SPARE, 1), 0.0
    )
    return first + second


def along_z_kernel(field_ref, cos_ref, sin_ref, out_ref):
    for group in range(4):
        field_re = field_ref[group, 64:192, :]
        field_im = field_ref[group, 0:128, :]
        waves = dot_nt(cos_ref[0], field_re) + dot_nt(cos_ref[1], field_re)
        first, second = spread_last(waves[256:272], 16)
        extra = jnp.concatenate([first, second, jnp.zeros((224, 128), F32)], 0)
        waves = waves[:256] + dot_nt(sin_ref[0], field_im) + dot_nt(sin_ref[1], field_im) + extra
        out_ref[:, group] = waves.reshape(16, 16, 128)


def line_waves(table, pair, sign):
    both = jnp.concatenate(pair, 1)
    high = both.astype(BF16)
    if both.dtype == BF16:
        stacked = jnp.concatenate([high, high], 0)
    else:
        low = (both - high.astype(F32)).astype(BF16)
        stacked = jnp.concatenate([high, high, low], 0)
    product = dot(table[:, : stacked.shape[0]], stacked)
    upper = lane_index(32) < 64
    result = []
    for lane in (0, 128):
        crossed = pltpu.roll(product[32:, lane : lane + 128], 64, 1)
        result.append(
            product[:32, lane : lane + 128] + jnp.where(upper, sign * crossed, -sign * crossed)
        )
    return result


def plane_kernel(sign, scale, copies, data_ref, table_ref, out_ref, middle_ref, end_ref):
    table = table_ref[...]
    for x in range(0, NB, 2):
        pair = [data_ref[2 * i : 2 * i + 2].reshape(32, 128) for i in (x, x + 1)]
        for i, rows in enumerate(line_waves(table, pair, sign)):
            middle_ref[(x + i) * 32 : (x + i + 1) * 32, :] = rows
    for y in range(0, NB, 2):
        pair = [middle_ref[pl.ds(i, 32, stride=32), :] for i in (y, y + 1)]
        for i, rows in enumerate(line_waves(table, pair, sign)):
            end_ref[pl.ds(y + i, 32, stride=32), :] = rows
    total = (end_ref[...] * scale).astype(BF16).reshape(64, 16, 128)
    for copy in range(copies):
        out_ref[:, copy] = total


def frequency_kernel(
    spec_ref, kernel_ref, select_ref, back_ref, out_ref, left_ref, right_ref, local_ref
):
    step = pl.program_id(0)

    @pl.when(step == 0)
    def _():
        total = jnp.zeros((512, 512), F32)
        last = jnp.zeros((32, 512), F32)
        for group in range(4):
            panel = spec_ref[:, :, group].reshape(512, 128)
            total += dot(panel, select_ref[group])
            closing = gather_last(panel[0:32].astype(F32), panel[32:64].astype(F32), 32)
            last += dot(closing.astype(BF16), select_ref[group])
        for kz in range(KZ):
            for rhs in range(RHS):
                row = (kz * RHS + rhs) * 16
                rows = total[row : row + 16] if kz < 16 else last[rhs * 16 : rhs * 16 + 16]
                for ref, lane in ((left_ref, 0), (right_ref, 128)):
                    re = rows[:, lane : lane + 128]
                    im = rows[:, 256 + lane : 384 + lane]
                    for slot, value in ((0, re), (2, im), (4, -im), (6, re)):
                        ref[pl.ds(kz * 8 + slot + rhs, 16, stride=8 * KZ), :] = value

    for kz in range(KZ):
        row = pl.multiple_of(step * (8 * KZ) + kz * 8, 8)
        panel = jnp.concatenate(
            [left_ref[pl.ds(row, 8), :], right_ref[pl.ds(row, 8), :]], 1
        ).astype(BF16)[:, :152]
        first = dot_nt(panel, kernel_ref[0, 0, 0, kz])
        second = dot_nt(panel, kernel_ref[1, 0, 0, kz])
        local_ref[pl.ds(row, 8), 0:76] = first + pltpu.roll(second, 4, 0)

    @pl.when(step == 15)
    def _():
        keep = lane_index(16) < 76
        for rhs in range(RHS):
            rows = []
            for kz in range(KZ):
                weight = 1.0 if kz in (0, 16) else 2.0
                parts = []
                for slot in (rhs, 2 + rhs):
                    part = local_ref[pl.ds(kz * 8 + slot, 16, stride=8 * KZ), :]
                    parts.append(jnp.where(keep, part * weight, 0.0))
                rows.append(jnp.concatenate(parts, 1).astype(BF16))
            rows = jnp.concatenate(rows, 0)
            for half in range(2):
                chunk = dot(rows, back_ref[half])
                first, second = spread_last(chunk[256:272], 16)
                extra = jnp.concatenate([first, second, jnp.zeros((224, 128), F32)], 0)
                chunk = chunk[:256] + extra
                out_ref[:, rhs * 2 + half] = chunk.astype(BF16).reshape(16, 16, 128)


def from_z_kernel(scale, data_ref, cos_ref, sin_ref, out_ref):
    for group in range(4):
        data = data_ref[:, group].reshape(256, 128)
        last = gather_last(data[0:16].astype(F32), data[16:32].astype(F32), 16)
        full = jnp.concatenate([data, last.astype(BF16)], 0)
        straight = dot_tn(full, cos_ref[0])
        crossed = dot_tn(data, sin_ref[0])
        total = (straight[0:HALF] + crossed[64 : 64 + HALF]) * scale
        half = group % 2
        out_ref[group // 2, half * HALF : half * HALF + HALF, :] = total


def vmem(count):
    return [pl.BlockSpec(memory_space=pltpu.VMEM)] * count


def along_z(field, cos, sin):
    return pl.pallas_call(
        along_z_kernel,
        out_shape=jax.ShapeDtypeStruct((16, 4, 16, 128), F32),
        in_specs=vmem(3),
        out_specs=pl.BlockSpec(memory_space=pltpu.VMEM),
        name="along_z",
    )(field, cos, sin)


def planes(data, table, sign, scale, copies, name):
    return pl.pallas_call(
        functools.partial(plane_kernel, sign, scale, copies),
        out_shape=jax.ShapeDtypeStruct((64, copies, 16, 128), BF16),
        in_specs=vmem(2),
        out_specs=pl.BlockSpec(memory_space=pltpu.VMEM),
        scratch_shapes=[pltpu.VMEM((1024, 128), F32), pltpu.VMEM((1024, 128), F32)],
        name=name,
    )(data, table)


def frequencies(spectrum, kernel, select, back):
    return pl.pallas_call(
        frequency_kernel,
        grid=(16,),
        out_shape=jax.ShapeDtypeStruct((16, 4, 16, 128), BF16),
        in_specs=[
            pl.BlockSpec((16, 2, 4, 16, 128), lambda i: (0, 0, 0, 0, 0)),
            pl.BlockSpec((2, 1, 1, KZ, 76, 152), lambda i: (0, 0, i, 0, 0, 0)),
            pl.BlockSpec((4, 128, 512), lambda i: (0, 0, 0)),
            pl.BlockSpec((2, 256, 128), lambda i: (0, 0, 0)),
        ],
        out_specs=pl.BlockSpec((16, 4, 16, 128), lambda i: (0, 0, 0, 0)),
        scratch_shapes=[
            pltpu.VMEM((16 * KZ * 8, 128), F32),
            pltpu.VMEM((16 * KZ * 8, 128), F32),
            pltpu.VMEM((16 * KZ * 8, 128), F32),
        ],
        name="frequencies",
    )(spectrum, kernel, select, back)


def from_z(data, cos, sin, scale):
    return pl.pallas_call(
        functools.partial(from_z_kernel, scale),
        out_shape=jax.ShapeDtypeStruct((2, 76, 512), F32),
        in_specs=vmem(3),
        out_specs=pl.BlockSpec(memory_space=pltpu.VMEM),
        name="from_z",
    )(data, cos, sin)


def exchange(chunks, axes):
    return lax.all_to_all(chunks, axes, 0, 0, tiled=True)


def on_device(multipoles, kernel):
    cos_z, sin_z = (jnp.asarray(t) for t in tables_z())
    table = jnp.asarray(table_line())
    near = ("bx", "by")
    field = jnp.pad(multipoles.reshape(4, HALF, 512), ((0, 0), (64, 192 - 64 - HALF), (0, 0)))
    waves = along_z(field, cos_z, sin_z).reshape(64, 16, 128)
    waves = exchange(waves, near)
    spectrum = planes(waves, table, 1.0, 1.0 / SCALE**3, 2, "to_waves")
    spectrum = exchange(spectrum.reshape(128, 16, 128), ("bx", "by", "col"))
    local = frequencies(
        spectrum.reshape(16, 2, 4, 16, 128),
        kernel,
        jnp.asarray(select_in()),
        jnp.asarray(select_out()),
    )
    local = exchange(local.reshape(64, 16, 128), near)
    back = planes(local, table, -1.0, 1.0 / (1024 * SCALE**2), 1, "from_waves")
    back = exchange(back.reshape(64, 16, 128), near)
    result = from_z(back.reshape(16, 4, 16, 128), cos_z, sin_z, 1.0 / (32 * SCALE))
    return result.reshape(multipoles.shape)


def solution(mesh):
    placed = (P(None, "col", "bx", "by"), P(None, "bx", "by", None, "col", None))
    return jax.shard_map(
        on_device, mesh=mesh, in_specs=placed, out_specs=P(None, "col", "bx", "by"), check_vma=False
    )
```

time: 251 us -> 125 us (0.50)
  blocking collectives: 148 us -> 64.5 us
  local copies, waits for them, and re-layouts: 64.4 us -> 24.3 us
  matrix products: 33.9 us -> 0 us
  Pallas kernels: 0 us -> 30.4 us
    all_to_all x7 -> x3, blocking collectives: 118 us -> 64.5 us  [exchange(): return lax.all_to_all(chunks, axes, 0, 0, tiled=True)]
    dot_general x24 -> x0, matrix products: 33.9 us -> none  [the longest x20 13.8 us: contract(): return jnp.einsum(pattern, values, table, precision=precise)]
    pallas_call x0 -> x5, Pallas kernels: none -> 30.4 us  [the longest x1 18.1 us: frequencies(): pl.pallas_call(frequency_kernel, grid=(16,), out_shape=jax.ShapeDtypeStru...]
    all_gather x1 -> x0, blocking collectives: 29.5 us -> none  [apply_kernel(): panels = lax.all_gather(spectrum, 'col', axis=2, tiled=True)]
    unnamed x11 -> x4, local copies, waits for them, and re-layouts: 41.8 us -> 21.3 us
    slice x3 -> x0, local copies, waits for them, and re-layouts: 15.7 us -> none  [the longest x1 15.2 us: kernel_terms(): kernel_part[0]]
    another operation x3 -> x0, local copies, waits for them, and re-layouts: 3.15 us -> none  [the longest x1 2.23 us: on_device(): spectrum = jnp.stack([spec_re, spec_im]).astype(jnp.bfloat16)]
    all_to_all x5 -> x0, local copies, waits for them, and re-layouts: 2.72 us -> none  [the longest x1 1.62 us: to_columns(): lax.all_to_all(waves, 'bx', split_axis=3, concat_axis=5, tiled=True)]
  transfers between devices with their start and end apart: 1 -> 1, of which waited for: 0 -> 0; matrix products, arithmetic and copies ran while one was open for 21% -> 16% of each run, Pallas kernels for 0% -> 0%
where the time goes in v1:
time: 125 us; the launch traced here: 124 us
  blocking collectives  64.5 us (52%)
  Pallas kernels  30.4 us (24%)
  local copies, waits for them, and re-layouts  24.3 us (19%)
  starting transfers between devices  4.75 us (4%)
    all_to_all x3, blocking collectives, exchange(): return lax.all_to_all(chunks, axes, 0, 0, tiled=True)  64.5 us
    unnamed x4, local copies, waits for them, and re-layouts  21.3 us
    pallas_call x1, Pallas kernels, frequencies(): pl.pallas_call(frequency_kernel, grid=(16,), out_shape=jax.ShapeDtypeStru...  18.1 us
    pallas_call x2, Pallas kernels, planes(): pl.pallas_call(functools.partial(plane_kernel, sign, scale, copies), out_...  6.08 us
    all_to_all x1, starting transfers between devices, exchange(): return lax.all_to_all(chunks, axes, 0, 0, tiled=True)  4.75 us
    pallas_call x1, Pallas kernels, along_z(): pl.pallas_call(along_z_kernel, out_shape=jax.ShapeDtypeStruct((16, 4, 16,...  3.53 us
    pallas_call x1, Pallas kernels, from_z(): pl.pallas_call(functools.partial(from_z_kernel, scale), out_shape=jax.Sha...  2.66 us
  transfers between devices with their start and end apart: 1, of which 0 were waited for; matrix products, arithmetic and copies ran while one was open for 16% of the time, Pallas kernels for 0%

profile of v1, /device:TPU:1, one launch (start us, length us, event | category | flops | bytes accessed | tf_op | source)
XLA Modules:
  0.0 123.9 jit_solution(12902389375722481230)
XLA Ops:
  0.0 0.9 copy.11
  1.0 1.0 pad.4.field_ref
  1.9 3.5 %along_z.1 = f32[16,4,16,128]{3,2,1,0:T(8,128)} custom-call(bf16[4,192,512]{2,1,0:T(8,128)(2,1)} %pad.4.field_ref, bf16[2,272,512]{2,1,0:T(8,128)(2,1)} %constant.13.clone.cos_ref, bf16[2,256,512]{2,1,0:T(8,128)(2,1)} %constant.14.clone.sin_ref), custom_call_target="tpu_custom_call" | custom-call | tf_op jit(solution)/shard_map/along_z/pallas_call | solution.py:231
  5.5 25.8 %all_to_all.20.data_ref = f32[64,16,128]{2,1,0:T(8,128)} all-to-all(f32[64,16,128]{2,1,0:T(8,128)} %bitcast.11), channel_id=1, replica_groups=mesh['bx'=32,'by'=2,'col'=2] {'bx','by'}, dimensions={0} | all-to-all | bytes 1048576 | tf_op jit(solution)/shard_map/all_to_all | solution.py:283
  31.3 3.2 %to_waves.1 = bf16[64,2,16,128]{3,2,1,0:T(8,128)(2,1)} custom-call(f32[64,16,128]{2,1,0:T(8,128)} %all_to_all.20.data_ref, bf16[64,96]{1,0:T(8,128)(2,1)} %constant.15.clone.table_ref), custom_call_target="tpu_custom_call" | custom-call | tf_op jit(solution)/shard_map/to_waves/pallas_call | solution.py:241
  34.4 4.7 %all-to-all-start.1 = ((bf16[128,16,128]{2,1,0:T(8,128)(2,1)}), bf16[128,16,128]{2,1,0:T(8,128)(2,1)S(1)}, u32[]{:S(2)}, u32[]{:S(2)}) async-start(bf16[128,16,128]{2,1,0:T(8,128)(2,1)} %bitcast.10), calls=%async_computation.1 | async-start | bytes 1048576 | tf_op jit(solution)/shard_map/all_to_all | solution.py:283
  39.2 19.5 %copy.12.kernel_ref = bf16[2,1,16,17,76,152]{5,4,3,2,1,0:T(8,128)(2,1)} copy(bf16[2,1,16,17,76,152]{5,2,4,3,1,0:T(8,128)(2,1)} %param.8) | data formatting | bytes 25137152 | tf_op args[1]
  58.7 0.0 all-to-all-done.1
  58.7 0.0 copy-start
  58.7 0.8 copy-done
  59.5 18.1 %frequencies.1 = bf16[16,4,16,128]{3,2,1,0:T(8,128)(2,1)} custom-call(bf16[16,2,4,16,128]{4,3,2,1,0:T(8,128)(2,1)} %bitcast.9, bf16[2,1,16,17,76,152]{5,4,3,2,1,0:T(8,128)(2,1)} %copy.12.kernel_ref, bf16[4,128,512]{2,1,0:T(8,128)(2,1)} %constant.16.clone.select_ref, bf16[2,256,128]{2,1,0:T(8,128)(2,1)} %constant.17.clone.back_ref), custom_call_target="tpu_custom_call" | custom-call | tf_op jit(solution)/shard_map/frequencies/pallas_call | solution.py:252
  77.6 21.9 %all_to_all.21.data_ref = bf16[64,16,128]{2,1,0:T(8,128)(2,1)} all-to-all(bf16[64,16,128]{2,1,0:T(8,128)(2,1)} %bitcast.13), channel_id=1, replica_groups=mesh['bx'=32,'by'=2,'col'=2] {'bx','by'}, dimensions={0} | all-to-all | bytes 524288 | tf_op jit(solution)/shard_map/all_to_all | solution.py:283
  99.6 2.9 %from_waves.1 = bf16[64,1,16,128]{3,2,1,0:T(8,128)(2,1)} custom-call(bf16[64,16,128]{2,1,0:T(8,128)(2,1)} %all_to_all.21.data_ref, bf16[64,96]{1,0:T(8,128)(2,1)} %constant.15.clone.table_ref), custom_call_target="tpu_custom_call" | custom-call | tf_op jit(solution)/shard_map/from_waves/pallas_call | solution.py:241
  102.5 16.7 %all_to_all.22 = bf16[64,16,128]{2,1,0:T(8,128)(2,1)} all-to-all(bf16[64,16,128]{2,1,0:T(8,128)(2,1)} %bitcast.15), channel_id=1, replica_groups=mesh['bx'=32,'by'=2,'col'=2] {'bx','by'}, dimensions={0} | all-to-all | bytes 524288 | tf_op jit(solution)/shard_map/all_to_all | solution.py:283
  119.2 2.7 %from_z.1 = f32[2,76,512]{2,1,0:T(8,128)} custom-call(bf16[16,4,16,128]{3,2,1,0:T(8,128)(2,1)} %bitcast.14, bf16[2,272,512]{2,1,0:T(8,128)(2,1)} %constant.13.clone.cos_ref, bf16[2,256,512]{2,1,0:T(8,128)(2,1)} %constant.14.clone.sin_ref), custom_call_target="tpu_custom_call" | custom-call | tf_op jit(solution)/shard_map/from_z/pallas_call | solution.py:273
  121.9 2.0 %copy.13 = f32[2,76,1,512]{3,2,1,0:T(1,128)} copy(f32[2,76,1,512]{3,1,0,2:T(8,128)} %bitcast.12) | data formatting | bytes 622592 | tf_op jit(solution)/shard_map/reshape | solution.py:305
  (1 shorter events, 0.0 us)
Async XLA Ops:
  34.4 24.3 %all-to-all-start.1 = ((bf16[128,16,128]{2,1,0:T(8,128)(2,1)}), bf16[128,16,128]{2,1,0:T(8,128)(2,1)S(1)}, u32[]{:S(2)}, u32[]{:S(2)}) async-start(bf16[128,16,128]{2,1,0:T(8,128)(2,1)} %bitcast.10), calls=%async_computation.1 | async-start | bytes 1048576 | tf_op jit(solution)/shard_map/all_to_all | solution.py:283
  58.7 0.8 copy-start

commit v2 on v1

v2 whole, which is shorter than its diff:
```python
import functools
import math

import jax
import jax.numpy as jnp
import numpy as np
from jax import lax
from jax.experimental import pallas as pl
from jax.experimental.pallas import tpu as pltpu
from jax.sharding import PartitionSpec as P

NB = 32
KZ = 17
RHS = 2
HALF = 38
SPARE = 19
F32 = jnp.float32
BF16 = jnp.bfloat16


def to_bf16(values):
    return np.asarray(values, np.float32).astype(jnp.bfloat16)


def table_scale():
    level = np.cos(2 * np.pi * np.arange(8) / 32)
    weight = np.array([2.0] + [4.0] * 7)
    scales = np.linspace(1.0, 2.0, 20001)[:-1]
    scaled = scales[:, None] * level[None, :]
    error = to_bf16(scaled).astype(np.float64) / scales[:, None] - level[None, :]
    return float(scales[np.argmin((weight * error**2).sum(1))])


SCALE = table_scale()


def split(table):
    high = to_bf16(SCALE * table)
    return high, to_bf16(SCALE * table - high.astype(np.float64))


def tables_z():
    kz = np.arange(KZ)[:, None]
    z = np.arange(NB)[None, :]
    angle = 2 * np.pi * ((kz * z) % NB) / NB
    eye = np.eye(8)
    cos = np.einsum("kz,ab->kabz", np.cos(angle), eye).reshape(KZ * 8, 8 * NB)
    sin = np.einsum("kz,ab->kabz", -np.sin(angle), eye).reshape(KZ * 8, 8 * NB)
    sin[128:] = 0
    cos_high, cos_low = split(cos)
    sin_high, sin_low = split(sin)
    ahead = np.concatenate([cos_high, cos_low, sin_high[:128], sin_low[:128]], 0)
    return ahead, np.concatenate([cos_high, sin_high], 1)


def table_line():
    k = np.arange(NB)
    angle = 2 * np.pi * ((k[:, None] * k[None, :]) % NB) / NB
    high, low = split(np.concatenate([np.cos(angle), np.sin(angle)]))
    return np.concatenate([high, low, high], 1)


def select_in():
    table = np.zeros((4, 128, 512), np.float32)
    c = np.arange(HALF)
    for half in range(2):
        for column in range(2):
            target = column * 76 + half * HALF + c
            table[half * 2 + column, c, target] = 1
            table[half * 2 + column, 64 + c, 256 + target] = 1
    return to_bf16(table)


def select_out():
    table = np.zeros((76, 16, 2, 128), np.float32)
    c = np.arange(HALF)
    for half in range(2):
        table[half * HALF + c, :, half, c] = 1
    return to_bf16(table.reshape(76 * 16, 256))


def lane_index(rows):
    return lax.broadcasted_iota(jnp.int32, (rows, 128), 1)


def lanes_between(rows, low, high):
    lane = lane_index(rows) % 64
    return (lane >= low) & (lane < high)


def dot_nt(left, right):
    return lax.dot_general(left, right, (((1,), (1,)), ((), ())), preferred_element_type=F32)


def dot_tn(left, right):
    return lax.dot_general(left, right, (((0,), (0,)), ((), ())), preferred_element_type=F32)


def dot(left, right):
    return jnp.dot(left, right, preferred_element_type=F32)


def spread_last(last, rows, base=0):
    spare = lanes_between(rows, HALF, HALF + SPARE)
    first = jnp.where(spare, pltpu.roll(last, (HALF - base) % 128, 1), 0.0)
    second = jnp.where(spare, pltpu.roll(last, (HALF - SPARE - base) % 128, 1), 0.0)
    return first, second


def gather_last(first, second, rows):
    first = jnp.where(lanes_between(rows, 0, SPARE), pltpu.roll(first, 128 - HALF, 1), 0.0)
    second = jnp.where(
        lanes_between(rows, SPARE, HALF), pltpu.roll(second, 128 - HALF + SPARE, 1), 0.0
    )
    return first + second


def along_z_kernel(field_ref, table_ref, out_ref, padded_ref):
    padded_ref[...] = jnp.zeros_like(padded_ref)
    for group in range(4):
        padded_ref[group * 64 : group * 64 + HALF, :] = field_ref[group]
    lower = lane_index(128) < 64
    spare = lanes_between(8, HALF, HALF + SPARE) & (lane_index(8) < 64)
    for block in range(2):
        product = dot_nt(table_ref[...], padded_ref[:, block * 256 : block * 256 + 256])
        cos = product[0:136] + product[136:272]
        sin = product[272:400] + product[400:528]
        for group in range(4):
            tile = slice(group // 2 * 128, group // 2 * 128 + 128)
            re, im, last = cos[:128, tile], sin[:, tile], cos[128:, tile]
            if group % 2 == 0:
                im = pltpu.roll(im, 64, 1)
            else:
                re = pltpu.roll(re, 64, 1)
            chunk = jnp.where(lower, re, im).reshape(16, 8, 128)
            first, second = spread_last(last, 8, group % 2 * 64)
            rows = slice(block * 8, block * 8 + 8)
            out_ref[:, group, rows, :] = chunk
            out_ref[0, group, rows, :] = chunk[0] + jnp.where(spare, first, 0.0)
            out_ref[1, group, rows, :] = chunk[1] + jnp.where(spare, second, 0.0)


def line_waves(table, pair, sign):
    both = jnp.concatenate(pair, 1)
    high = both.astype(BF16)
    if both.dtype == BF16:
        stacked = jnp.concatenate([high, high], 0)
    else:
        low = (both - high.astype(F32)).astype(BF16)
        stacked = jnp.concatenate([high, high, low], 0)
    product = dot(table[:, : stacked.shape[0]], stacked)
    upper = lane_index(32) < 64
    result = []
    for lane in (0, 128):
        crossed = pltpu.roll(product[32:, lane : lane + 128], 64, 1)
        result.append(
            product[:32, lane : lane + 128] + jnp.where(upper, sign * crossed, -sign * crossed)
        )
    return result


def plane_kernel(sign, scale, copies, data_ref, table_ref, out_ref, middle_ref, end_ref):
    table = table_ref[...]
    for x in range(0, NB, 2):
        pair = [data_ref[2 * i : 2 * i + 2].reshape(32, 128) for i in (x, x + 1)]
        for i, rows in enumerate(line_waves(table, pair, sign)):
            middle_ref[(x + i) * 32 : (x + i + 1) * 32, :] = rows
    for y in range(0, NB, 2):
        pair = [middle_ref[pl.ds(i, 32, stride=32), :] for i in (y, y + 1)]
        for i, rows in enumerate(line_waves(table, pair, sign)):
            end_ref[pl.ds(y + i, 32, stride=32), :] = rows
    total = (end_ref[...] * scale).astype(BF16).reshape(64, 16, 128)
    for copy in range(copies):
        out_ref[:, copy] = total


def frequency_kernel(spec_ref, kernel_ref, select_ref, back_ref, out_ref, panel_ref):
    step = pl.program_id(0)

    @pl.when(step == 0)
    def _():
        total = jnp.zeros((512, 512), F32)
        last = jnp.zeros((32, 512), F32)
        for group in range(4):
            panel = spec_ref[:, :, group].reshape(512, 128)
            total += dot(panel, select_ref[group])
            closing = gather_last(panel[0:32].astype(F32), panel[32:64].astype(F32), 32)
            last += dot(closing.astype(BF16), select_ref[group])
        for kz in range(KZ):
            for rhs in range(RHS):
                row = (kz * RHS + rhs) * 16
                rows = total[row : row + 16] if kz < 16 else last[rhs * 16 : rhs * 16 + 16]
                re, im = rows[:, :256].astype(BF16), rows[:, 256:].astype(BF16)
                upper = slice(rhs * 16, rhs * 16 + 16)
                lower = slice(32 + rhs * 16, 48 + rhs * 16)
                panel_ref[kz, upper, 0:256] = re
                panel_ref[kz, lower, 0:256] = im
                panel_ref[kz, upper, 256:512] = -im
                panel_ref[kz, lower, 256:512] = re

    panel = panel_ref[step]
    product = dot_nt(panel[:, 0:152], kernel_ref[0, 0, 0].reshape(1216, 152))
    product += dot_nt(panel[:, 256:408], kernel_ref[1, 0, 0].reshape(1216, 152))
    row = lax.broadcasted_iota(jnp.int32, (64, 1216), 0)
    lane = lax.broadcasted_iota(jnp.int32, (64, 1216), 1)
    own = jnp.where(row % 16 == lane % 16, product, 0.0).astype(BF16)
    weight = jnp.where((step == 0) | (step == 16), 1.0, 2.0).astype(F32)
    local = dot(own, back_ref[...]) * weight
    chunks = []
    for rhs in range(RHS):
        for half in range(2):
            tile = local[:, half * 128 : half * 128 + 128]
            im = pltpu.roll(tile[32 + rhs * 16 : 48 + rhs * 16], 64, 1)
            chunks.append(tile[rhs * 16 : rhs * 16 + 16] + im)

    @pl.when(step < 16)
    def _():
        for group in range(4):
            out_ref[step, group] = chunks[group].astype(BF16)

    @pl.when(step == 16)
    def _():
        for group in range(4):
            for block, extra in enumerate(spread_last(chunks[group], 16)):
                whole = out_ref[block, group].astype(F32) + extra
                out_ref[block, group] = whole.astype(BF16)


def from_z_kernel(scale, data_ref, table_ref, out_ref):
    for group in range(4):
        data = data_ref[:, group].astype(F32)
        first_row = (group // 2 * 76 + group % 2 * HALF) * 4
        for block in range(2):
            rows = data[:, block * 8 : block * 8 + 8, :].reshape(128, 128)
            last = gather_last(rows[0:8], rows[8:16], 8)
            full = jnp.concatenate([rows, last], 0).astype(BF16)
            product = dot_tn(full, table_ref[...])
            total = (product[0:HALF, :256] + product[64 : 64 + HALF, 256:]) * scale
            for part in range(2):
                start = first_row + block * 2 + part
                out_ref[pl.ds(start, HALF, stride=4), :] = total[:, part * 128 : part * 128 + 128]


def vmem(count):
    return [pl.BlockSpec(memory_space=pltpu.VMEM)] * count


def grant(mib):
    return pltpu.CompilerParams(vmem_limit_bytes=mib * 2**20)


def along_z(field, table):
    return pl.pallas_call(
        along_z_kernel,
        out_shape=jax.ShapeDtypeStruct((16, 4, 16, 128), F32),
        in_specs=vmem(2),
        out_specs=pl.BlockSpec(memory_space=pltpu.VMEM),
        scratch_shapes=[pltpu.VMEM((256, 512), BF16)],
        compiler_params=grant(8),
        name="along_z",
    )(field, table)


def planes(data, table, sign, scale, copies, name):
    return pl.pallas_call(
        functools.partial(plane_kernel, sign, scale, copies),
        out_shape=jax.ShapeDtypeStruct((64, copies, 16, 128), BF16),
        in_specs=vmem(2),
        out_specs=pl.BlockSpec(memory_space=pltpu.VMEM),
        scratch_shapes=[pltpu.VMEM((1024, 128), F32), pltpu.VMEM((1024, 128), F32)],
        compiler_params=grant(8),
        name=name,
    )(data, table)


def frequencies(spectrum, kernel, select, back):
    return pl.pallas_call(
        frequency_kernel,
        grid=(KZ,),
        out_shape=jax.ShapeDtypeStruct((16, 4, 16, 128), BF16),
        in_specs=[
            pl.BlockSpec((16, 2, 4, 16, 128), lambda i: (0, 0, 0, 0, 0)),
            pl.BlockSpec((2, 1, 1, 76, 16, 152), lambda i: (0, 0, i, 0, 0, 0)),
            pl.BlockSpec((4, 128, 512), lambda i: (0, 0, 0)),
            pl.BlockSpec((1216, 256), lambda i: (0, 0)),
        ],
        out_specs=pl.BlockSpec((16, 4, 16, 128), lambda i: (0, 0, 0, 0)),
        scratch_shapes=[pltpu.VMEM((KZ, 64, 512), BF16)],
        compiler_params=grant(16),
        name="frequencies",
    )(spectrum, kernel, select, back)


def from_z(data, table, scale):
    return pl.pallas_call(
        functools.partial(from_z_kernel, scale),
        out_shape=jax.ShapeDtypeStruct((608, 128), F32),
        in_specs=vmem(2),
        out_specs=pl.BlockSpec(memory_space=pltpu.VMEM),
        compiler_params=grant(8),
        name="from_z",
    )(data, table)


def exchange(chunks, axes):
    return lax.all_to_all(chunks, axes, 0, 0, tiled=True)


def on_device(multipoles, kernel):
    ahead, behind = (jnp.asarray(t) for t in tables_z())
    table = jnp.asarray(table_line())
    near = ("bx", "by")
    waves = along_z(multipoles.reshape(4, HALF, 512), ahead).reshape(64, 16, 128)
    waves = exchange(waves, near)
    spectrum = planes(waves, table, 1.0, 1.0 / SCALE**3, 2, "to_waves")
    spectrum = exchange(spectrum.reshape(128, 16, 128), ("bx", "by", "col"))
    local = frequencies(
        spectrum.reshape(16, 2, 4, 16, 128),
        kernel.transpose(0, 1, 3, 4, 2, 5),
        jnp.asarray(select_in()),
        jnp.asarray(select_out()),
    )
    local = exchange(local.reshape(64, 16, 128), near)
    back = planes(local, table, -1.0, 1.0 / (1024 * SCALE**2), 1, "from_waves")
    back = exchange(back.reshape(64, 16, 128), near)
    result = from_z(back.reshape(16, 4, 16, 128), behind, 1.0 / (32 * SCALE))
    return result.reshape(multipoles.shape)


def solution(mesh):
    placed = (P(None, "col", "bx", "by"), P(None, "bx", "by", None, "col", None))
    return jax.shard_map(
        on_device, mesh=mesh, in_specs=placed, out_specs=P(None, "col", "bx", "by"), check_vma=False
    )
```

time: 125 us -> 106 us (0.85)
  local copies, waits for them, and re-layouts: 24.3 us -> 11.8 us
  Pallas kernels: 30.4 us -> 19.2 us
  blocking collectives: 64.5 us -> 74.7 us
  starting transfers between devices: 4.75 us -> 0 us
    all_to_all x3 -> x4, blocking collectives: 64.5 us -> 74.7 us  [exchange(): return lax.all_to_all(chunks, axes, 0, 0, tiled=True)]
    unnamed x4 -> x15, local copies, waits for them, and re-layouts: 21.3 us -> 11.8 us
    all_to_all x1 -> x0, starting transfers between devices: 4.75 us -> none  [exchange(): return lax.all_to_all(chunks, axes, 0, 0, tiled=True)]
    pallas_call x2, Pallas kernels: 6.08 us -> 2.53 us  [planes(): pl.pallas_call(functools.partial(plane_kernel, sign, scale, copies), out_...]
    pallas_call x1, Pallas kernels: 18.1 us -> 14.9 us  [frequencies(): pl.pallas_call(frequency_kernel, grid=(KZ,), out_shape=jax.ShapeDtypeStru...]
    pallas_call x1, Pallas kernels: 3.53 us -> 0.45 us  [along_z(): pl.pallas_call(along_z_kernel, out_shape=jax.ShapeDtypeStruct((16, 4, 16,...]
    reshape x1 -> x0, local copies, waits for them, and re-layouts: 2.01 us -> none  [on_device(): return result.reshape(multipoles.shape)]
    pallas_call x1, Pallas kernels: 2.66 us -> 1.34 us  [from_z(): pl.pallas_call(functools.partial(from_z_kernel, scale), out_shape=jax.Sha...]
  transfers between devices with their start and end apart: 1 -> 0, of which waited for: 0 -> 0; matrix products, arithmetic and copies ran while one was open for 16% -> 0% of each run, Pallas kernels for 0% -> 0%
where the time goes in v2:
time: 106 us
  blocking collectives  74.7 us (70%)
  Pallas kernels  19.2 us (18%)
  local copies, waits for them, and re-layouts  11.8 us (11%)
    all_to_all x4, blocking collectives, exchange(): return lax.all_to_all(chunks, axes, 0, 0, tiled=True)  74.7 us
    pallas_call x1, Pallas kernels, frequencies(): pl.pallas_call(frequency_kernel, grid=(KZ,), out_shape=jax.ShapeDtypeStru...  14.9 us
    unnamed x15, local copies, waits for them, and re-layouts  11.8 us
    pallas_call x2, Pallas kernels, planes(): pl.pallas_call(functools.partial(plane_kernel, sign, scale, copies), out_...  2.53 us

profile of v2, /device:TPU:1, one launch (start us, length us, event | category | flops | bytes accessed | tf_op | source)
XLA Modules:
  0.0 105.8 jit_solution(14801149978080696227)
XLA Ops:
  0.0 0.0 copy-start.6
  0.0 0.0 copy-start.4
  0.0 1.0 copy.10
  1.0 0.0 copy-start.3
  1.0 0.9 copy-done.3
  2.0 0.5 along_z.1
  2.4 25.5 %all_to_all.20.data_ref = f32[64,16,128]{2,1,0:T(8,128)S(1)} all-to-all(f32[64,16,128]{2,1,0:T(8,128)S(1)} %bitcast.12), channel_id=1, replica_groups=mesh['bx'=32,'by'=2,'col'=2] {'bx','by'}, dimensions={0} | all-to-all | bytes 1048576 | tf_op jit(solution)/shard_map/all_to_all | solution.py:306
  27.9 0.0 copy-start.5
  27.9 0.7 copy-done.5
  28.7 1.3 %to_waves.1 = bf16[64,2,16,128]{3,2,1,0:T(8,128)(2,1)S(1)} custom-call(f32[64,16,128]{2,1,0:T(8,128)S(1)} %all_to_all.20.data_ref, bf16[64,96]{1,0:T(8,128)(2,1)S(1)} %copy-done.5), custom_call_target="tpu_custom_call" | custom-call | tf_op jit(solution)/shard_map/to_waves/pallas_call | solution.py:265
  29.9 18.4 %all_to_all.21 = bf16[128,16,128]{2,1,0:T(8,128)(2,1)S(1)} all-to-all(bf16[128,16,128]{2,1,0:T(8,128)(2,1)S(1)} %bitcast.13), channel_id=1, replica_groups=mesh['bx'=32,'by'=2,'col'=2] {'bx','by','col'}, dimensions={0} | all-to-all | bytes 1048576 | tf_op jit(solution)/shard_map/all_to_all | solution.py:306
  48.3 0.0 copy-start
  48.3 7.0 %copy-done = bf16[2,1,16,17,76,152]{5,2,4,3,1,0:T(8,128)(2,1)S(1)} copy-done((bf16[2,1,16,17,76,152]{5,2,4,3,1,0:T(8,128)(2,1)S(1)}, bf16[2,1,16,17,76,152]{5,2,4,3,1,0:T(8,128)(2,1)}, u32[]{:S(2)}) %copy-start) | copy-done | bytes 12568600
  55.3 0.0 copy-start.1
  55.3 1.1 %copy-done.1 = bf16[1216,256]{1,0:T(8,128)(2,1)S(1)} copy-done((bf16[1216,256]{1,0:T(8,128)(2,1)S(1)}, bf16[1216,256]{1,0:T(8,128)(2,1)}, u32[]{:S(2)}) %copy-start.1) | copy-done | bytes 622616
  56.4 0.0 copy-start.2
  56.4 1.0 copy-done.2
  57.4 14.9 %frequencies.1 = bf16[16,4,16,128]{3,2,1,0:T(8,128)(2,1)S(1)} custom-call(bf16[16,2,4,16,128]{4,3,2,1,0:T(8,128)(2,1)S(1)} %bitcast.11, bf16[2,1,17,76,16,152]{5,4,3,2,1,0:T(8,128)(2,1)S(1)} %bitcast.10, bf16[4,128,512]{2,1,0:T(8,128)(2,1)S(1)} %copy-done.2, bf16[1216,256]{1,0:T(8,128)(2,1)S(1)} %copy-done.1), custom_call_target="tpu_custom_call" | custom-call | tf_op jit(solution)/shard_map/frequencies/pallas_call | solution.py:277
  72.3 15.3 %all_to_all.22.data_ref = bf16[64,16,128]{2,1,0:T(8,128)(2,1)S(1)} all-to-all(bf16[64,16,128]{2,1,0:T(8,128)(2,1)S(1)} %bitcast.14), channel_id=1, replica_groups=mesh['bx'=32,'by'=2,'col'=2] {'bx','by'}, dimensions={0} | all-to-all | bytes 524288 | tf_op jit(solution)/shard_map/all_to_all | solution.py:306
  87.6 0.0 copy-done.6
  87.6 1.3 %from_waves.1 = bf16[64,1,16,128]{3,2,1,0:T(8,128)(2,1)S(1)} custom-call(bf16[64,16,128]{2,1,0:T(8,128)(2,1)S(1)} %all_to_all.22.data_ref, bf16[64,96]{1,0:T(8,128)(2,1)S(1)} %copy-done.6), custom_call_target="tpu_custom_call" | custom-call | tf_op jit(solution)/shard_map/from_waves/pallas_call | solution.py:265
  88.9 15.6 %all_to_all.23 = bf16[64,16,128]{2,1,0:T(8,128)(2,1)S(1)} all-to-all(bf16[64,16,128]{2,1,0:T(8,128)(2,1)S(1)} %bitcast.15), channel_id=1, replica_groups=mesh['bx'=32,'by'=2,'col'=2] {'bx','by'}, dimensions={0} | all-to-all | bytes 524288 | tf_op jit(solution)/shard_map/all_to_all | solution.py:306
  104.4 0.0 copy-done.4
  104.5 1.3 %from_z.1 = f32[608,128]{1,0:T(8,128)} custom-call(bf16[16,4,16,128]{3,2,1,0:T(8,128)(2,1)S(1)} %bitcast.16, bf16[136,512]{1,0:T(8,128)(2,1)S(1)} %copy-done.4), custom_call_target="tpu_custom_call" | custom-call | tf_op jit(solution)/shard_map/from_z/pallas_call | solution.py:295
  (1 shorter events, 0.0 us)
Async XLA Ops:
  0.0 87.6 %copy-start.6 = (bf16[64,96]{1,0:T(8,128)(2,1)S(1)}, bf16[64,96]{1,0:T(8,128)(2,1)}, u32[]{:S(2)}) copy-start(bf16[64,96]{1,0:T(8,128)(2,1)} %constant.12.clone.table_ref) | copy-start | bytes 36868
  0.0 104.4 %copy-start.4 = (bf16[136,512]{1,0:T(8,128)(2,1)S(1)}, bf16[136,512]{1,0:T(8,128)(2,1)}, u32[]{:S(2)}) copy-start(bf16[136,512]{1,0:T(8,128)(2,1)} %constant.11.clone.table_ref) | copy-start | bytes 417796
  1.0 1.0 copy-start.3
  27.9 0.7 copy-start.5
  48.3 7.0 %copy-start = (bf16[2,1,16,17,76,152]{5,2,4,3,1,0:T(8,128)(2,1)S(1)}, bf16[2,1,16,17,76,152]{5,2,4,3,1,0:T(8,128)(2,1)}, u32[]{:S(2)}) copy-start(bf16[2,1,16,17,76,152]{5,2,4,3,1,0:T(8,128)(2,1)} %param.8) | copy-start | bytes 37705732
  55.3 1.1 %copy-start.1 = (bf16[1216,256]{1,0:T(8,128)(2,1)S(1)}, bf16[1216,256]{1,0:T(8,128)(2,1)}, u32[]{:S(2)}) copy-start(bf16[1216,256]{1,0:T(8,128)(2,1)} %constant.14.clone.back_ref) | copy-start | bytes 1867780
  56.4 1.0 copy-start.2

commit v3 on v2

v3 whole, which is shorter than its diff:
```python
import functools
import math

import jax
import jax.numpy as jnp
import numpy as np
from jax import lax
from jax.experimental import pallas as pl
from jax.experimental.pallas import tpu as pltpu
from jax.sharding import PartitionSpec as P

NB = 32
KZ = 17
RHS = 2
HALF = 38
SPARE = 19
BATCHES = (10, 7)
F32 = jnp.float32
BF16 = jnp.bfloat16


def to_bf16(values):
    return np.asarray(values, np.float32).astype(jnp.bfloat16)


def table_scale():
    level = np.cos(2 * np.pi * np.arange(8) / 32)
    weight = np.array([2.0] + [4.0] * 7)
    scales = np.linspace(1.0, 2.0, 20001)[:-1]
    scaled = scales[:, None] * level[None, :]
    error = to_bf16(scaled).astype(np.float64) / scales[:, None] - level[None, :]
    return float(scales[np.argmin((weight * error**2).sum(1))])


SCALE = table_scale()


def table_back():
    kz = np.arange(KZ)[:, None]
    z = np.arange(NB)[None, :]
    angle = 2 * np.pi * ((kz * z) % NB) / NB
    eye = np.eye(8)
    cos = np.einsum("kz,ab->kabz", np.cos(angle), eye).reshape(KZ * 8, 8 * NB)
    sin = np.einsum("kz,ab->kabz", -np.sin(angle), eye).reshape(KZ * 8, 8 * NB)
    sin[128:] = 0
    return to_bf16(SCALE * np.concatenate([cos, sin], 1))


def iota(shape, axis):
    return lax.broadcasted_iota(jnp.int32, shape, axis)


def cosine(steps):
    return SCALE * jnp.cos((steps % NB).astype(F32) * (2 * math.pi / NB))


def high_part(values):
    return values.astype(BF16).astype(F32)


def line_table():
    row, lane = iota((64, 128), 0), iota((64, 128), 1)
    values = cosine((row % NB) * (lane % NB) - 8 * (row // NB))
    high = high_part(values)
    return jnp.where(lane // NB == 1, values - high, high).astype(BF16)


def ahead_table():
    kz, z = iota((24, 128), 0), iota((24, 128), 1) % NB
    cos = cosine(kz * z)
    sin = cosine(kz * z + 8)
    parts = [(high_part(cos), KZ), (cos - high_part(cos), KZ)]
    parts += [(high_part(sin), 16), (sin - high_part(sin), 16)]
    sides = []
    for side in range(2):
        own = iota((KZ, 8, 128), 1) == iota((KZ, 8, 128), 2) // NB + 4 * side
        blocks = []
        for values, count in parts:
            spread = jnp.broadcast_to(values[:count, None, :], (count, 8, 128))
            blocks.append(jnp.where(own[:count], spread, 0.0).reshape(count * 8, 128))
        sides.append(jnp.concatenate(blocks, 0).astype(BF16))
    return jnp.concatenate(sides, 1)


def select_in(group):
    start = group % 2 * 76 + group // 2 * HALF
    row, lane = iota((128, 512), 0), iota((128, 512), 1)
    real = (row < HALF) & (lane == row + start)
    imag = (row >= 64) & (row < 64 + HALF) & (lane == row + (192 + start))
    return jnp.where(real | imag, 1.0, 0.0).astype(BF16)


def select_out():
    coefficient, lane = iota((1216, 256), 0) // 16, iota((1216, 256), 1)
    target = jnp.where(coefficient < HALF, coefficient, coefficient + 128 - HALF)
    return jnp.where(lane == target, 1.0, 0.0).astype(BF16)


def lane_index(rows):
    return lax.broadcasted_iota(jnp.int32, (rows, 128), 1)


def lanes_between(rows, low, high):
    lane = lane_index(rows) % 64
    return (lane >= low) & (lane < high)


def dot_nt(left, right):
    return lax.dot_general(left, right, (((1,), (1,)), ((), ())), preferred_element_type=F32)


def dot_tn(left, right):
    return lax.dot_general(left, right, (((0,), (0,)), ((), ())), preferred_element_type=F32)


def dot(left, right):
    return jnp.dot(left, right, preferred_element_type=F32)


def spread_last(last, rows, base=0):
    spare = lanes_between(rows, HALF, HALF + SPARE)
    first = jnp.where(spare, pltpu.roll(last, (HALF - base) % 128, 1), 0.0)
    second = jnp.where(spare, pltpu.roll(last, (HALF - SPARE - base) % 128, 1), 0.0)
    return first, second


def gather_last(first, second, rows):
    first = jnp.where(lanes_between(rows, 0, SPARE), pltpu.roll(first, 128 - HALF, 1), 0.0)
    second = jnp.where(
        lanes_between(rows, SPARE, HALF), pltpu.roll(second, 128 - HALF + SPARE, 1), 0.0
    )
    return first + second


def along_z_kernel(field_ref, out_ref, padded_ref):
    table = ahead_table()
    padded_ref[...] = jnp.zeros_like(padded_ref)
    field = field_ref[...].astype(F32)
    for group in range(4):
        half = group % 2 * HALF
        rows = field[half : half + HALF, group // 2, :]
        padded_ref[group * 64 : group * 64 + HALF, :] = rows.astype(BF16)
    lower = lane_index(128) < 64
    spare = lanes_between(8, HALF, HALF + SPARE) & (lane_index(8) < 64)
    for block in range(2):
        product = dot_nt(table, padded_ref[:, block * 256 : block * 256 + 256])
        cos = product[0:136] + product[136:272]
        sin = product[272:400] + product[400:528]
        for group in range(4):
            tile = slice(group // 2 * 128, group // 2 * 128 + 128)
            re, im, last = cos[:128, tile], sin[:, tile], cos[128:, tile]
            if group % 2 == 0:
                im = pltpu.roll(im, 64, 1)
            else:
                re = pltpu.roll(re, 64, 1)
            chunk = jnp.where(lower, re, im).reshape(16, 8, 128)
            first, second = spread_last(last, 8, group % 2 * 64)
            rows = slice(block * 8, block * 8 + 8)
            out_ref[:, group, rows, :] = chunk
            out_ref[0, group, rows, :] = chunk[0] + jnp.where(spare, first, 0.0)
            out_ref[1, group, rows, :] = chunk[1] + jnp.where(spare, second, 0.0)


def line_waves(table, pair, sign):
    both = jnp.concatenate(pair, 1)
    high = both.astype(BF16)
    if both.dtype == BF16:
        stacked = jnp.concatenate([high, high], 0)
    else:
        low = (both - high.astype(F32)).astype(BF16)
        stacked = jnp.concatenate([high, high, low], 0)
    product = dot(table[:, : stacked.shape[0]], stacked)
    upper = lane_index(32) < 64
    result = []
    for lane in (0, 128):
        crossed = pltpu.roll(product[32:, lane : lane + 128], 64, 1)
        result.append(
            product[:32, lane : lane + 128] + jnp.where(upper, sign * crossed, -sign * crossed)
        )
    return result


def plane_kernel(sign, scale, copies, data_ref, out_ref, middle_ref, end_ref):
    table = line_table()
    for x in range(0, NB, 2):
        pair = [data_ref[2 * i : 2 * i + 2].reshape(32, 128) for i in (x, x + 1)]
        for i, rows in enumerate(line_waves(table, pair, sign)):
            middle_ref[(x + i) * 32 : (x + i + 1) * 32, :] = rows
    for y in range(0, NB, 2):
        pair = [middle_ref[pl.ds(i, 32, stride=32), :] for i in (y, y + 1)]
        for i, rows in enumerate(line_waves(table, pair, sign)):
            end_ref[pl.ds(y + i, 32, stride=32), :] = rows
    total = (end_ref[...] * scale).astype(BF16).reshape(64, 16, 128)
    for copy in range(copies):
        out_ref[:, copy] = total


def panels(spec_ref, panel_ref):
    total = jnp.zeros((512, 512), F32)
    last = jnp.zeros((32, 512), F32)
    for group in range(4):
        panel = spec_ref[:, :, group].reshape(512, 128)
        select = select_in(group)
        total += dot(panel, select)
        closing = gather_last(panel[0:32].astype(F32), panel[32:64].astype(F32), 32)
        last += dot(closing.astype(BF16), select)
    for kz in range(KZ):
        for rhs in range(RHS):
            row = (kz * RHS + rhs) * 16
            rows = total[row : row + 16] if kz < 16 else last[rhs * 16 : rhs * 16 + 16]
            re, im = rows[:, :256].astype(BF16), rows[:, 256:].astype(BF16)
            upper = slice(rhs * 16, rhs * 16 + 16)
            lower = slice(32 + rhs * 16, 48 + rhs * 16)
            panel_ref[kz, upper, 0:256] = re
            panel_ref[kz, lower, 0:256] = im
            panel_ref[kz, upper, 256:512] = -im
            panel_ref[kz, lower, 256:512] = re


def frequency_kernel(
    spec_ref, kernel_hbm, out_ref, back_ref, kernel_ref, panel_ref, own_ref, kernel_sem
):
    def load(kz):
        return pltpu.make_async_copy(
            kernel_hbm.at[:, 0, kz], kernel_ref.at[kz], kernel_sem.at[kz]
        )

    for kz in range(KZ):
        load(kz).start()
    panels(spec_ref, panel_ref)
    back_ref[...] = select_out()

    row = lax.broadcasted_iota(jnp.int32, (64, 128), 0)
    lane = lax.broadcasted_iota(jnp.int32, (64, 128), 1)
    same = row % 16 == lane % 16

    def step(kz, carry):
        load(kz).wait()
        panel = panel_ref[kz]
        product = dot_nt(panel[:, 0:152], kernel_ref[kz, 0].reshape(1216, 152))
        product += dot_nt(panel[:, 256:408], kernel_ref[kz, 1].reshape(1216, 152))
        for tile in range(0, 1216, 128):
            wide = min(128, 1216 - tile)
            part = jnp.where(same[:, :wide], product[:, tile : tile + wide], 0.0)
            own_ref[kz, :, tile : tile + wide] = part.astype(BF16)
        return carry

    def finish(first, count):
        local = dot(own_ref[first : first + count].reshape(count * 64, 1216), back_ref[...])
        local = local.reshape(count, 64, 256)
        for kz in range(first, first + count):
            for group in range(4):
                rhs, half = group // 2, group % 2
                tile = local[kz - first, :, half * 128 : half * 128 + 128]
                im = pltpu.roll(tile[32 + rhs * 16 : 48 + rhs * 16], 64, 1)
                chunk = tile[rhs * 16 : rhs * 16 + 16] + im
                if kz in (0, 16):
                    chunk = chunk.astype(BF16)
                else:
                    chunk = (chunk * 2.0).astype(BF16)
                if kz < 16:
                    out_ref[kz, group] = chunk
                else:
                    for block, extra in enumerate(spread_last(chunk.astype(F32), 16)):
                        whole = out_ref[block, group].astype(F32) + extra
                        out_ref[block, group] = whole.astype(BF16)

    first = 0
    for count in BATCHES:
        lax.fori_loop(first, first + count, step, 0)
        finish(first, count)
        first += count


def from_z_kernel(scale, data_ref, table_ref, out_ref):
    for group in range(4):
        data = data_ref[:, group].astype(F32)
        first_row = (group // 2 * 76 + group % 2 * HALF) * 4
        for block in range(2):
            rows = data[:, block * 8 : block * 8 + 8, :].reshape(128, 128)
            last = gather_last(rows[0:8], rows[8:16], 8)
            full = jnp.concatenate([rows, last], 0).astype(BF16)
            product = dot_tn(full, table_ref[...])
            total = (product[0:HALF, :256] + product[64 : 64 + HALF, 256:]) * scale
            for part in range(2):
                start = first_row + block * 2 + part
                out_ref[pl.ds(start, HALF, stride=4), :] = total[:, part * 128 : part * 128 + 128]


def vmem(count):
    return [pl.BlockSpec(memory_space=pltpu.VMEM)] * count


def grant(mib):
    return pltpu.CompilerParams(vmem_limit_bytes=mib * 2**20)


def along_z(field):
    return pl.pallas_call(
        along_z_kernel,
        out_shape=jax.ShapeDtypeStruct((16, 4, 16, 128), F32),
        in_specs=vmem(1),
        out_specs=pl.BlockSpec(memory_space=pltpu.VMEM),
        scratch_shapes=[pltpu.VMEM((256, 512), BF16)],
        compiler_params=grant(8),
        name="along_z",
    )(field)


def planes(data, sign, scale, copies, name):
    return pl.pallas_call(
        functools.partial(plane_kernel, sign, scale, copies),
        out_shape=jax.ShapeDtypeStruct((64, copies, 16, 128), BF16),
        in_specs=vmem(1),
        out_specs=pl.BlockSpec(memory_space=pltpu.VMEM),
        scratch_shapes=[pltpu.VMEM((1024, 128), F32), pltpu.VMEM((1024, 128), F32)],
        compiler_params=grant(8),
        name=name,
    )(data)


def frequencies(spectrum, kernel):
    return pl.pallas_call(
        frequency_kernel,
        out_shape=jax.ShapeDtypeStruct((16, 4, 16, 128), BF16),
        in_specs=vmem(1) + [pl.BlockSpec(memory_space=pltpu.HBM)],
        out_specs=pl.BlockSpec(memory_space=pltpu.VMEM),
        scratch_shapes=[
            pltpu.VMEM((1216, 256), BF16),
            pltpu.VMEM((KZ, 2, 76, 16, 152), BF16),
            pltpu.VMEM((KZ, 64, 512), BF16),
            pltpu.VMEM((KZ, 64, 1216), BF16),
            pltpu.SemaphoreType.DMA((KZ,)),
        ],
        compiler_params=grant(40),
        name="frequencies",
    )(spectrum, kernel)


def from_z(data, table, scale):
    return pl.pallas_call(
        functools.partial(from_z_kernel, scale),
        out_shape=jax.ShapeDtypeStruct((608, 128), F32),
        in_specs=vmem(2),
        out_specs=pl.BlockSpec(memory_space=pltpu.VMEM),
        compiler_params=grant(8),
        name="from_z",
    )(data, table)


def exchange(chunks, axes):
    return lax.all_to_all(chunks, axes, 0, 0, tiled=True)


def on_device(multipoles, kernel):
    near = ("bx", "by")
    waves = along_z(multipoles[:, :, 0, :].transpose(1, 0, 2)).reshape(64, 16, 128)
    waves = exchange(waves, near)
    spectrum = planes(waves, 1.0, 1.0 / SCALE**3, 2, "to_waves")
    spectrum = exchange(spectrum.reshape(128, 16, 128), ("bx", "by", "col"))
    local = frequencies(spectrum.reshape(16, 2, 4, 16, 128), kernel.transpose(0, 1, 3, 4, 2, 5))
    local = exchange(local.reshape(64, 16, 128), near)
    back = planes(local, -1.0, 1.0 / (1024 * SCALE**2), 1, "from_waves")
    back = exchange(back.reshape(64, 16, 128), near)
    behind = jnp.asarray(table_back())
    result = from_z(back.reshape(16, 4, 16, 128), behind, 1.0 / (32 * SCALE))
    return result.reshape(multipoles.shape)


def solution(mesh):
    placed = (P(None, "col", "bx", "by"), P(None, "bx", "by", None, "col", None))
    return jax.shard_map(
        on_device, mesh=mesh, in_specs=placed, out_specs=P(None, "col", "bx", "by"), check_vma=False
    )
```

time: 106 us -> 92.5 us (0.87)
  local copies, waits for them, and re-layouts: 11.8 us -> 0.92 us
  Pallas kernels: 19.2 us -> 16.7 us
    unnamed x15 -> x4, local copies, waits for them, and re-layouts: 11.8 us -> 0.92 us
    pallas_call x1, Pallas kernels: 14.9 us -> 11.6 us  [frequencies(): pl.pallas_call(frequency_kernel, out_shape=jax.ShapeDtypeStruct((16, 4, 1...]
where the time goes in v3:
time: 92.5 us; the launch traced here: 92.3 us
  blocking collectives  74.7 us (81%)
  Pallas kernels  16.7 us (18%)
    all_to_all x4, blocking collectives, exchange(): return lax.all_to_all(chunks, axes, 0, 0, tiled=True)  74.7 us
    pallas_call x1, Pallas kernels, frequencies(): pl.pallas_call(frequency_kernel, out_shape=jax.ShapeDtypeStruct((16, 4, 1...  11.6 us
    pallas_call x2, Pallas kernels, planes(): pl.pallas_call(functools.partial(plane_kernel, sign, scale, copies), out_...  2.83 us

profile of v3, /device:TPU:1, one launch (start us, length us, event | category | flops | bytes accessed | tf_op | source)
XLA Modules:
  0.0 92.3 jit_solution(5066626372403553909)
XLA Ops:
  0.0 0.0 copy-start
  0.0 0.9 copy-done
  0.9 0.0 copy-start.1
  0.9 0.9 along_z.1
  1.8 25.5 %all_to_all.20.data_ref = f32[64,16,128]{2,1,0:T(8,128)S(1)} all-to-all(f32[64,16,128]{2,1,0:T(8,128)S(1)} %bitcast.13), channel_id=1, replica_groups=mesh['bx'=32,'by'=2,'col'=2] {'bx','by'}, dimensions={0} | all-to-all | bytes 1048576 | tf_op jit(solution)/shard_map/all_to_all | solution.py:352
  27.3 1.4 %to_waves.1 = bf16[64,2,16,128]{3,2,1,0:T(8,128)(2,1)S(1)} custom-call(f32[64,16,128]{2,1,0:T(8,128)S(1)} %all_to_all.20.data_ref), custom_call_target="tpu_custom_call" | custom-call | tf_op jit(solution)/shard_map/to_waves/pallas_call | solution.py:311
  28.7 18.4 %all_to_all.21 = bf16[128,16,128]{2,1,0:T(8,128)(2,1)S(1)} all-to-all(bf16[128,16,128]{2,1,0:T(8,128)(2,1)S(1)} %bitcast.12), channel_id=1, replica_groups=mesh['bx'=32,'by'=2,'col'=2] {'bx','by','col'}, dimensions={0} | all-to-all | bytes 1048576 | tf_op jit(solution)/shard_map/all_to_all | solution.py:352
  47.1 11.6 %frequencies.1 = bf16[16,4,16,128]{3,2,1,0:T(8,128)(2,1)S(1)} custom-call(bf16[16,2,4,16,128]{4,3,2,1,0:T(8,128)(2,1)S(1)} %bitcast.11, bf16[2,1,17,76,16,152]{5,4,3,2,1,0:T(8,128)(2,1)} %bitcast.18), custom_call_target="tpu_custom_call" | custom-call | tf_op jit(solution)/shard_map/frequencies/pallas_call | solution.py:323
  58.7 15.3 %all_to_all.22.data_ref = bf16[64,16,128]{2,1,0:T(8,128)(2,1)S(1)} all-to-all(bf16[64,16,128]{2,1,0:T(8,128)(2,1)S(1)} %bitcast.14), channel_id=1, replica_groups=mesh['bx'=32,'by'=2,'col'=2] {'bx','by'}, dimensions={0} | all-to-all | bytes 524288 | tf_op jit(solution)/shard_map/all_to_all | solution.py:352
  74.0 1.4 %from_waves.1 = bf16[64,1,16,128]{3,2,1,0:T(8,128)(2,1)S(1)} custom-call(bf16[64,16,128]{2,1,0:T(8,128)(2,1)S(1)} %all_to_all.22.data_ref), custom_call_target="tpu_custom_call" | custom-call | tf_op jit(solution)/shard_map/from_waves/pallas_call | solution.py:311
  75.4 15.6 %all_to_all.23 = bf16[64,16,128]{2,1,0:T(8,128)(2,1)S(1)} all-to-all(bf16[64,16,128]{2,1,0:T(8,128)(2,1)S(1)} %bitcast.15), channel_id=1, replica_groups=mesh['bx'=32,'by'=2,'col'=2] {'bx','by'}, dimensions={0} | all-to-all | bytes 524288 | tf_op jit(solution)/shard_map/all_to_all | solution.py:352
  91.0 0.0 copy-done.1
  91.0 1.3 %from_z.1 = f32[608,128]{1,0:T(8,128)} custom-call(bf16[16,4,16,128]{3,2,1,0:T(8,128)(2,1)S(1)} %bitcast.16, bf16[136,512]{1,0:T(8,128)(2,1)S(1)} %copy-done.1), custom_call_target="tpu_custom_call" | custom-call | tf_op jit(solution)/shard_map/from_z/pallas_call | solution.py:341
Async XLA Ops:
  0.0 0.9 copy-start
  0.9 90.0 %copy-start.1 = (bf16[136,512]{1,0:T(8,128)(2,1)S(1)}, bf16[136,512]{1,0:T(8,128)(2,1)}, u32[]{:S(2)}) copy-start(bf16[136,512]{1,0:T(8,128)(2,1)} %constant.2.clone.table_ref) | copy-start | bytes 417796

commit v4 on v3

--- a/solution.py
+++ b/solution.py
@@ -14,6 +14,7 @@
 RHS = 2
 HALF = 38
 SPARE = 19
+ROWS = 3
 BATCHES = (10, 7)
 F32 = jnp.float32
 BF16 = jnp.bfloat16
@@ -66,28 +67,20 @@
 
 
 def ahead_table():
-    kz, z = iota((24, 128), 0), iota((24, 128), 1) % NB
-    cos = cosine(kz * z)
-    sin = cosine(kz * z + 8)
-    parts = [(high_part(cos), KZ), (cos - high_part(cos), KZ)]
-    parts += [(high_part(sin), 16), (sin - high_part(sin), 16)]
-    sides = []
-    for side in range(2):
-        own = iota((KZ, 8, 128), 1) == iota((KZ, 8, 128), 2) // NB + 4 * side
-        blocks = []
-        for values, count in parts:
-            spread = jnp.broadcast_to(values[:count, None, :], (count, 8, 128))
-            blocks.append(jnp.where(own[:count], spread, 0.0).reshape(count * 8, 128))
-        sides.append(jnp.concatenate(blocks, 0).astype(BF16))
-    return jnp.concatenate(sides, 1)
-
-
-def select_in(group):
-    start = group % 2 * 76 + group // 2 * HALF
-    row, lane = iota((128, 512), 0), iota((128, 512), 1)
-    real = (row < HALF) & (lane == row + start)
-    imag = (row >= 64) & (row < 64 + HALF) & (lane == row + (192 + start))
-    return jnp.where(real | imag, 1.0, 0.0).astype(BF16)
+    row, lane = iota((128, 128), 0), iota((128, 128), 1)
+    place = lane % 64
+    own = (place < ROWS * KZ) & (place // KZ == row // NB)
+    values = jnp.where(own, cosine((place % KZ) * (row % NB) + 8 * (lane // 64)), 0.0)
+    high = high_part(values)
+    return high.astype(BF16), (values - high).astype(BF16)
+
+
+def select_in():
+    line, lane = iota((128 * ROWS, 512), 0), iota((128 * ROWS, 512), 1)
+    source = line % 128
+    row = source // 2 * ROWS + line // 128
+    target = row // 76 * 256 + source % 2 * 76 + row % 76
+    return jnp.where((row < 152) & (lane == target), 1.0, 0.0).astype(BF16)
 
 
 def select_out():
@@ -132,33 +125,25 @@
     return first + second
 
 
-def along_z_kernel(field_ref, out_ref, padded_ref):
-    table = ahead_table()
-    padded_ref[...] = jnp.zeros_like(padded_ref)
+def spread_rows_kernel(field_ref, out_ref, rows_ref, chunk_ref):
     field = field_ref[...].astype(F32)
-    for group in range(4):
-        half = group % 2 * HALF
-        rows = field[half : half + HALF, group // 2, :]
-        padded_ref[group * 64 : group * 64 + HALF, :] = rows.astype(BF16)
-    lower = lane_index(128) < 64
-    spare = lanes_between(8, HALF, HALF + SPARE) & (lane_index(8) < 64)
-    for block in range(2):
-        product = dot_nt(table, padded_ref[:, block * 256 : block * 256 + 256])
-        cos = product[0:136] + product[136:272]
-        sin = product[272:400] + product[400:528]
-        for group in range(4):
-            tile = slice(group // 2 * 128, group // 2 * 128 + 128)
-            re, im, last = cos[:128, tile], sin[:, tile], cos[128:, tile]
-            if group % 2 == 0:
-                im = pltpu.roll(im, 64, 1)
-            else:
-                re = pltpu.roll(re, 64, 1)
-            chunk = jnp.where(lower, re, im).reshape(16, 8, 128)
-            first, second = spread_last(last, 8, group % 2 * 64)
-            rows = slice(block * 8, block * 8 + 8)
-            out_ref[:, group, rows, :] = chunk
-            out_ref[0, group, rows, :] = chunk[0] + jnp.where(spare, first, 0.0)
-            out_ref[1, group, rows, :] = chunk[1] + jnp.where(spare, second, 0.0)
+    rows_ref[:, 152:168, :] = jnp.zeros((4, 16, 128), F32)
+    for tile in range(4):
+        for rhs in range(RHS):
+            part = field[:, rhs, tile * 128 : tile * 128 + 128]
+            rows_ref[tile, rhs * 76 : rhs * 76 + 76, :] = part
+    chunk_ref[896:1024, :] = jnp.zeros((128, 128), F32)
+    slot = lane_index(56) // NB
+    for tile in range(4):
+        parts = [rows_ref[tile, pl.ds(row, 56, stride=ROWS), :] for row in range(ROWS)]
+        for y in range(4):
+            total = jnp.zeros((56, 128), F32)
+            for row in range(ROWS):
+                shift = (row - y) % 4 * NB
+                moved = pltpu.roll(parts[row], shift, 1) if shift else parts[row]
+                total = jnp.where(slot == row, moved, total)
+            chunk_ref[pl.ds(tile * 4 + y, 56, stride=16), :] = total
+    out_ref[...] = chunk_ref[...].astype(BF16).reshape(64, 16, 128)
 
 
 def line_waves(table, pair, sign):
@@ -180,10 +165,10 @@
     return result
 
 
-def plane_kernel(sign, scale, copies, data_ref, out_ref, middle_ref, end_ref):
+def plane_waves(sign, scale, copies, load, out_ref, middle_ref, end_ref):
     table = line_table()
     for x in range(0, NB, 2):
-        pair = [data_ref[2 * i : 2 * i + 2].reshape(32, 128) for i in (x, x + 1)]
+        pair = [load(i) for i in (x, x + 1)]
         for i, rows in enumerate(line_waves(table, pair, sign)):
             middle_ref[(x + i) * 32 : (x + i + 1) * 32, :] = rows
     for y in range(0, NB, 2):
@@ -195,30 +180,75 @@
         out_ref[:, copy] = total
 
 
-def panels(spec_ref, panel_ref):
-    total = jnp.zeros((512, 512), F32)
-    last = jnp.zeros((32, 512), F32)
-    for group in range(4):
-        panel = spec_ref[:, :, group].reshape(512, 128)
-        select = select_in(group)
-        total += dot(panel, select)
-        closing = gather_last(panel[0:32].astype(F32), panel[32:64].astype(F32), 32)
-        last += dot(closing.astype(BF16), select)
-    for kz in range(KZ):
+def to_waves_kernel(data_ref, out_ref, start_ref, middle_ref, end_ref):
+    high, low = ahead_table()
+    data = data_ref[...].reshape(1024, 128)
+    start_ref[...] = dot(data, high) + dot(data, low)
+
+    def load(x):
+        return start_ref[x * 32 : x * 32 + 32, :]
+
+    plane_waves(1.0, 1.0 / SCALE**3, 2, load, out_ref, middle_ref, end_ref)
+
+
+def from_waves_kernel(data_ref, out_ref, middle_ref, end_ref):
+    def load(x):
+        return data_ref[2 * x : 2 * x + 2].reshape(32, 128)
+
+    plane_waves(-1.0, 1.0 / (1024 * SCALE**2), 1, load, out_ref, middle_ref, end_ref)
+
+
+def panels(spec_ref, panel_ref, flat_ref, line_ref, whole_ref):
+    flat_ref[...] = spec_ref[...].astype(F32).reshape(2048, 128)
+
+    def turn(ky, carry):
+        lanes = flat_ref[pl.ds(ky, 128, stride=16), :].T
+        for row in range(ROWS):
+            for part in range(2):
+                start = part * 64 + row * KZ
+                place = pl.multiple_of(ky * 48 + part * 24, 8)
+                line_ref[row, pl.ds(place, 24), :] = lanes[start : start + 24]
+        return carry
+
+    lax.fori_loop(0, 16, turn, 0)
+    select = select_in()
+    total = dot(line_ref[0].astype(BF16), select[0:128])
+    for row in range(1, ROWS):
+        total += dot(line_ref[row].astype(BF16), select[row * 128 : row * 128 + 128])
+    for tile in range(4):
+        whole_ref[tile] = total[:, tile * 128 : tile * 128 + 128]
+
+    def place_panel(kz, carry):
         for rhs in range(RHS):
-            row = (kz * RHS + rhs) * 16
-            rows = total[row : row + 16] if kz < 16 else last[rhs * 16 : rhs * 16 + 16]
-            re, im = rows[:, :256].astype(BF16), rows[:, 256:].astype(BF16)
             upper = slice(rhs * 16, rhs * 16 + 16)
             lower = slice(32 + rhs * 16, 48 + rhs * 16)
-            panel_ref[kz, upper, 0:256] = re
-            panel_ref[kz, lower, 0:256] = im
-            panel_ref[kz, upper, 256:512] = -im
-            panel_ref[kz, lower, 256:512] = re
+            for tile in range(2):
+                tiles = whole_ref.at[rhs * 2 + tile]
+                re = tiles[pl.ds(kz, 16, stride=48), :].astype(BF16)
+                im = tiles[pl.ds(kz + 24, 16, stride=48), :].astype(BF16)
+                near = slice(tile * 128, tile * 128 + 128)
+                far = slice(256 + tile * 128, 384 + tile * 128)
+                panel_ref[kz, upper, near] = re
+                panel_ref[kz, lower, near] = im
+                panel_ref[kz, upper, far] = -im
+                panel_ref[kz, lower, far] = re
+        return carry
+
+    lax.fori_loop(0, KZ, place_panel, 0)
 
 
 def frequency_kernel(
-    spec_ref, kernel_hbm, out_ref, back_ref, kernel_ref, panel_ref, own_ref, kernel_sem
+    spec_ref,
+    kernel_hbm,
+    out_ref,
+    back_ref,
+    kernel_ref,
+    panel_ref,
+    own_ref,
+    flat_ref,
+    line_ref,
+    whole_ref,
+    kernel_sem,
 ):
     def load(kz):
         return pltpu.make_async_copy(
@@ -227,7 +257,7 @@
 
     for kz in range(KZ):
         load(kz).start()
-    panels(spec_ref, panel_ref)
+    panels(spec_ref, panel_ref, flat_ref, line_ref, whole_ref)
     back_ref[...] = select_out()
 
     row = lax.broadcasted_iota(jnp.int32, (64, 128), 0)
@@ -295,28 +325,20 @@
     return pltpu.CompilerParams(vmem_limit_bytes=mib * 2**20)
 
 
-def along_z(field):
+def local_call(kernel, name, result, scratch, *operands):
     return pl.pallas_call(
-        along_z_kernel,
-        out_shape=jax.ShapeDtypeStruct((16, 4, 16, 128), F32),
-        in_specs=vmem(1),
+        kernel,
+        out_shape=result,
+        in_specs=vmem(len(operands)),
         out_specs=pl.BlockSpec(memory_space=pltpu.VMEM),
-        scratch_shapes=[pltpu.VMEM((256, 512), BF16)],
-        compiler_params=grant(8),
-        name="along_z",
-    )(field)
-
-
-def planes(data, sign, scale, copies, name):
-    return pl.pallas_call(
-        functools.partial(plane_kernel, sign, scale, copies),
-        out_shape=jax.ShapeDtypeStruct((64, copies, 16, 128), BF16),
-        in_specs=vmem(1),
-        out_specs=pl.BlockSpec(memory_space=pltpu.VMEM),
-        scratch_shapes=[pltpu.VMEM((1024, 128), F32), pltpu.VMEM((1024, 128), F32)],
+        scratch_shapes=[pltpu.VMEM(shape, F32) for shape in scratch],
         compiler_params=grant(8),
         name=name,
-    )(data)
+    )(*operands)
+
+
+def chunks_of(*shape):
+    return jax.ShapeDtypeStruct(shape, BF16)
 
 
 def frequencies(spectrum, kernel):
@@ -330,6 +352,9 @@
             pltpu.VMEM((KZ, 2, 76, 16, 152), BF16),
             pltpu.VMEM((KZ, 64, 512), BF16),
             pltpu.VMEM((KZ, 64, 1216), BF16),
+            pltpu.VMEM((2048, 128), F32),
+            pltpu.VMEM((ROWS, 768, 128), F32),
+            pltpu.VMEM((4, 768, 128), F32),
             pltpu.SemaphoreType.DMA((KZ,)),
         ],
         compiler_params=grant(40),
@@ -354,13 +379,21 @@
 
 def on_device(multipoles, kernel):
     near = ("bx", "by")
-    waves = along_z(multipoles[:, :, 0, :].transpose(1, 0, 2)).reshape(64, 16, 128)
-    waves = exchange(waves, near)
-    spectrum = planes(waves, 1.0, 1.0 / SCALE**3, 2, "to_waves")
+    plane = (1024, 128)
+    field = multipoles[:, :, 0, :].transpose(1, 0, 2)
+    rows = local_call(
+        spread_rows_kernel, "spread_rows", chunks_of(64, 16, 128), [(4, 168, 128), plane], field
+    )
+    rows = exchange(rows, near)
+    spectrum = local_call(
+        to_waves_kernel, "to_waves", chunks_of(64, 2, 16, 128), [plane, plane, plane], rows
+    )
     spectrum = exchange(spectrum.reshape(128, 16, 128), ("bx", "by", "col"))
-    local = frequencies(spectrum.reshape(16, 2, 4, 16, 128), kernel.transpose(0, 1, 3, 4, 2, 5))
+    local = frequencies(spectrum, kernel.transpose(0, 1, 3, 4, 2, 5))
     local = exchange(local.reshape(64, 16, 128), near)
-    back = planes(local, -1.0, 1.0 / (1024 * SCALE**2), 1, "from_waves")
+    back = local_call(
+        from_waves_kernel, "from_waves", chunks_of(64, 1, 16, 128), [plane, plane], local
+    )
     back = exchange(back.reshape(64, 16, 128), near)
     behind = jnp.asarray(table_back())
     result = from_z(back.reshape(16, 4, 16, 128), behind, 1.0 / (32 * SCALE))

time: 92.5 us -> 91.5 us (0.989)
  blocking collectives: 74.7 us -> 71.9 us
  Pallas kernels: 16.7 us -> 18.4 us
    all_to_all x4, blocking collectives: 74.7 us -> 71.9 us  [exchange(): return lax.all_to_all(chunks, axes, 0, 0, tiled=True)]
    pallas_call x1, Pallas kernels: 11.6 us -> 13.1 us  [frequencies(): pl.pallas_call(frequency_kernel, out_shape=jax.ShapeDtypeStruct((16, 4, 1...]
where the time goes in v4:
time: 91.5 us; the launch traced here: 91.2 us
  blocking collectives  71.9 us (79%)
  Pallas kernels  18.4 us (20%)
  local copies, waits for them, and re-layouts  0.92 us (1%)
    all_to_all x4, blocking collectives, exchange(): return lax.all_to_all(chunks, axes, 0, 0, tiled=True)  71.9 us
    pallas_call x1, Pallas kernels, frequencies(): pl.pallas_call(frequency_kernel, out_shape=jax.ShapeDtypeStruct((16, 4, 1...  13.1 us
    pallas_call x3, Pallas kernels, local_call(): pl.pallas_call(kernel, out_shape=result, in_specs=vmem(len(operands)), ou...  3.97 us

profile of v4, /device:TPU:1, one launch (start us, length us, event | category | flops | bytes accessed | tf_op | source)
XLA Modules:
  0.0 91.2 jit_solution(11424063375829130808)
XLA Ops:
  0.0 0.0 copy-start
  0.0 0.9 copy-done
  0.9 0.0 copy-start.1
  0.9 0.6 spread_rows.1
  1.5 23.2 %all_to_all.20.data_ref = bf16[64,16,128]{2,1,0:T(8,128)(2,1)S(1)} all-to-all(bf16[64,16,128]{2,1,0:T(8,128)(2,1)S(1)} %spread_rows.1), channel_id=1, replica_groups=mesh['bx'=32,'by'=2,'col'=2] {'bx','by'}, dimensions={0} | all-to-all | bytes 524288 | tf_op jit(solution)/shard_map/all_to_all | solution.py:377
  24.7 2.0 %to_waves.1 = bf16[64,2,16,128]{3,2,1,0:T(8,128)(2,1)S(1)} custom-call(bf16[64,16,128]{2,1,0:T(8,128)(2,1)S(1)} %all_to_all.20.data_ref), custom_call_target="tpu_custom_call" | custom-call | tf_op jit(solution)/shard_map/to_waves/pallas_call | solution.py:329
  26.7 17.9 %all_to_all.21.spec_ref = bf16[128,16,128]{2,1,0:T(8,128)(2,1)S(1)} all-to-all(bf16[128,16,128]{2,1,0:T(8,128)(2,1)S(1)} %bitcast.9), channel_id=1, replica_groups=mesh['bx'=32,'by'=2,'col'=2] {'bx','by','col'}, dimensions={0} | all-to-all | bytes 1048576 | tf_op jit(solution)/shard_map/all_to_all | solution.py:377
  44.6 13.1 %frequencies.1 = bf16[16,4,16,128]{3,2,1,0:T(8,128)(2,1)S(1)} custom-call(bf16[128,16,128]{2,1,0:T(8,128)(2,1)S(1)} %all_to_all.21.spec_ref, bf16[2,1,17,76,16,152]{5,4,3,2,1,0:T(8,128)(2,1)} %bitcast.14), custom_call_target="tpu_custom_call" | custom-call | tf_op jit(solution)/shard_map/frequencies/pallas_call | solution.py:345
  57.7 15.3 %all_to_all.22.data_ref = bf16[64,16,128]{2,1,0:T(8,128)(2,1)S(1)} all-to-all(bf16[64,16,128]{2,1,0:T(8,128)(2,1)S(1)} %bitcast.10), channel_id=1, replica_groups=mesh['bx'=32,'by'=2,'col'=2] {'bx','by'}, dimensions={0} | all-to-all | bytes 524288 | tf_op jit(solution)/shard_map/all_to_all | solution.py:377
  72.9 1.4 %from_waves.1 = bf16[64,1,16,128]{3,2,1,0:T(8,128)(2,1)S(1)} custom-call(bf16[64,16,128]{2,1,0:T(8,128)(2,1)S(1)} %all_to_all.22.data_ref), custom_call_target="tpu_custom_call" | custom-call | tf_op jit(solution)/shard_map/from_waves/pallas_call | solution.py:329
  74.3 15.6 %all_to_all.23 = bf16[64,16,128]{2,1,0:T(8,128)(2,1)S(1)} all-to-all(bf16[64,16,128]{2,1,0:T(8,128)(2,1)S(1)} %bitcast.11), channel_id=1, replica_groups=mesh['bx'=32,'by'=2,'col'=2] {'bx','by'}, dimensions={0} | all-to-all | bytes 524288 | tf_op jit(solution)/shard_map/all_to_all | solution.py:377
  89.9 0.0 copy-done.1
  89.9 1.3 %from_z.1 = f32[608,128]{1,0:T(8,128)} custom-call(bf16[16,4,16,128]{3,2,1,0:T(8,128)(2,1)S(1)} %bitcast.12, bf16[136,512]{1,0:T(8,128)(2,1)S(1)} %copy-done.1), custom_call_target="tpu_custom_call" | custom-call | tf_op jit(solution)/shard_map/from_z/pallas_call | solution.py:366
Async XLA Ops:
  0.0 0.9 %copy-start = (bf16[2,76,1,512]{3,0,2,1:T(2,128)(2,1)S(1)}, bf16[2,76,1,512]{3,0,2,1:T(2,128)(2,1)}, u32[]{:S(2)}) copy-start(bf16[2,76,1,512]{3,0,2,1:T(2,128)(2,1)} %param.3) | copy-start | bytes 466948
  0.9 89.0 %copy-start.1 = (bf16[136,512]{1,0:T(8,128)(2,1)S(1)}, bf16[136,512]{1,0:T(8,128)(2,1)}, u32[]{:S(2)}) copy-start(bf16[136,512]{1,0:T(8,128)(2,1)} %constant.2.clone.table_ref) | copy-start | bytes 417796

commit v5 on v4

--- a/solution.py
+++ b/solution.py
@@ -15,7 +15,6 @@
 HALF = 38
 SPARE = 19
 ROWS = 3
-BATCHES = (10, 7)
 F32 = jnp.float32
 BF16 = jnp.bfloat16
 
@@ -81,6 +80,14 @@
     row = source // 2 * ROWS + line // 128
     target = row // 76 * 256 + source % 2 * 76 + row % 76
     return jnp.where((row < 152) & (lane == target), 1.0, 0.0).astype(BF16)
+
+
+def pick_table():
+    line, lane = iota((144, 128), 0), iota((144, 128), 1)
+    block, kz = line // 24, line % 24
+    return jnp.where((kz < KZ) & (lane == block % 2 * 64 + block // 2 * KZ + kz), 1.0, 0.0).astype(
+        BF16
+    )
 
 
 def select_out():
@@ -198,43 +205,31 @@
     plane_waves(-1.0, 1.0 / (1024 * SCALE**2), 1, load, out_ref, middle_ref, end_ref)
 
 
-def panels(spec_ref, panel_ref, flat_ref, line_ref, whole_ref):
+def panels(spec_ref, panel_ref, flat_ref, line_ref):
     flat_ref[...] = spec_ref[...].astype(F32).reshape(2048, 128)
-
-    def turn(ky, carry):
-        lanes = flat_ref[pl.ds(ky, 128, stride=16), :].T
-        for row in range(ROWS):
-            for part in range(2):
-                start = part * 64 + row * KZ
-                place = pl.multiple_of(ky * 48 + part * 24, 8)
-                line_ref[row, pl.ds(place, 24), :] = lanes[start : start + 24]
-        return carry
-
-    lax.fori_loop(0, 16, turn, 0)
-    select = select_in()
-    total = dot(line_ref[0].astype(BF16), select[0:128])
-    for row in range(1, ROWS):
-        total += dot(line_ref[row].astype(BF16), select[row * 128 : row * 128 + 128])
-    for tile in range(4):
-        whole_ref[tile] = total[:, tile * 128 : tile * 128 + 128]
-
-    def place_panel(kz, carry):
+    pick = pick_table()
+    for ky in range(0, 16, 2):
+        both = [flat_ref[pl.ds(i, 128, stride=16), :] for i in (ky, ky + 1)]
+        turned = dot_nt(pick, jnp.concatenate(both, 0).astype(BF16))
+        for i in range(2):
+            for row in range(ROWS):
+                for part in range(2):
+                    block = turned[(row * 2 + part) * 24 : (row * 2 + part) * 24 + 24]
+                    place = pl.ds(part * 16 + ky + i, 24, stride=32)
+                    line_ref[row, place, :] = block[:, i * 128 : i * 128 + 128]
+    lines = [line_ref[row, 0 : KZ * 32, :].astype(BF16) for row in range(ROWS)]
+    total = dot(jnp.concatenate(lines, 1), select_in()).astype(BF16)
+    for kz in range(KZ):
+        re = total[kz * 32 : kz * 32 + 16]
+        im = total[kz * 32 + 16 : kz * 32 + 32]
         for rhs in range(RHS):
+            lanes = slice(rhs * 256, rhs * 256 + 256)
             upper = slice(rhs * 16, rhs * 16 + 16)
             lower = slice(32 + rhs * 16, 48 + rhs * 16)
-            for tile in range(2):
-                tiles = whole_ref.at[rhs * 2 + tile]
-                re = tiles[pl.ds(kz, 16, stride=48), :].astype(BF16)
-                im = tiles[pl.ds(kz + 24, 16, stride=48), :].astype(BF16)
-                near = slice(tile * 128, tile * 128 + 128)
-                far = slice(256 + tile * 128, 384 + tile * 128)
-                panel_ref[kz, upper, near] = re
-                panel_ref[kz, lower, near] = im
-                panel_ref[kz, upper, far] = -im
-                panel_ref[kz, lower, far] = re
-        return carry
-
-    lax.fori_loop(0, KZ, place_panel, 0)
+            panel_ref[kz, upper, 0:256] = re[:, lanes]
+            panel_ref[kz, lower, 0:256] = im[:, lanes]
+            panel_ref[kz, upper, 256:512] = -im[:, lanes]
+            panel_ref[kz, lower, 256:512] = re[:, lanes]
 
 
 def frequency_kernel(
@@ -247,7 +242,6 @@
     own_ref,
     flat_ref,
     line_ref,
-    whole_ref,
     kernel_sem,
 ):
     def load(kz):
@@ -257,15 +251,14 @@
 
     for kz in range(KZ):
         load(kz).start()
-    panels(spec_ref, panel_ref, flat_ref, line_ref, whole_ref)
+    panels(spec_ref, panel_ref, flat_ref, line_ref)
     back_ref[...] = select_out()
 
     row = lax.broadcasted_iota(jnp.int32, (64, 128), 0)
     lane = lax.broadcasted_iota(jnp.int32, (64, 128), 1)
     same = row % 16 == lane % 16
 
-    def step(kz, carry):
-        load(kz).wait()
+    def step(kz):
         panel = panel_ref[kz]
         product = dot_nt(panel[:, 0:152], kernel_ref[kz, 0].reshape(1216, 152))
         product += dot_nt(panel[:, 256:408], kernel_ref[kz, 1].reshape(1216, 152))
@@ -273,33 +266,33 @@
             wide = min(128, 1216 - tile)
             part = jnp.where(same[:, :wide], product[:, tile : tile + wide], 0.0)
             own_ref[kz, :, tile : tile + wide] = part.astype(BF16)
+
+    def pair(half, carry):
+        for kz in (2 * half, 2 * half + 1):
+            load(kz).wait()
+        for kz in (2 * half, 2 * half + 1):
+            step(kz)
         return carry
 
-    def finish(first, count):
-        local = dot(own_ref[first : first + count].reshape(count * 64, 1216), back_ref[...])
-        local = local.reshape(count, 64, 256)
-        for kz in range(first, first + count):
-            for group in range(4):
-                rhs, half = group // 2, group % 2
-                tile = local[kz - first, :, half * 128 : half * 128 + 128]
-                im = pltpu.roll(tile[32 + rhs * 16 : 48 + rhs * 16], 64, 1)
-                chunk = tile[rhs * 16 : rhs * 16 + 16] + im
-                if kz in (0, 16):
-                    chunk = chunk.astype(BF16)
-                else:
-                    chunk = (chunk * 2.0).astype(BF16)
-                if kz < 16:
-                    out_ref[kz, group] = chunk
-                else:
-                    for block, extra in enumerate(spread_last(chunk.astype(F32), 16)):
-                        whole = out_ref[block, group].astype(F32) + extra
-                        out_ref[block, group] = whole.astype(BF16)
-
-    first = 0
-    for count in BATCHES:
-        lax.fori_loop(first, first + count, step, 0)
-        finish(first, count)
-        first += count
+    lax.fori_loop(0, KZ // 2, pair, 0)
+    load(KZ - 1).wait()
+    step(KZ - 1)
+
+    local = dot(own_ref[...].reshape(KZ * 64, 1216), back_ref[...]).reshape(KZ, 64, 256)
+    for kz in range(KZ):
+        for group in range(4):
+            rhs, half = group // 2, group % 2
+            tile = local[kz, :, half * 128 : half * 128 + 128]
+            im = pltpu.roll(tile[32 + rhs * 16 : 48 + rhs * 16], 64, 1)
+            chunk = tile[rhs * 16 : rhs * 16 + 16] + im
+            if kz not in (0, 16):
+                chunk = chunk * 2.0
+            if kz < 16:
+                out_ref[kz, group] = chunk.astype(BF16)
+            else:
+                for block, extra in enumerate(spread_last(chunk, 16)):
+                    whole = out_ref[block, group].astype(F32) + extra
+                    out_ref[block, group] = whole.astype(BF16)
 
 
 def from_z_kernel(scale, data_ref, table_ref, out_ref):
@@ -354,7 +347,6 @@
             pltpu.VMEM((KZ, 64, 1216), BF16),
             pltpu.VMEM((2048, 128), F32),
             pltpu.VMEM((ROWS, 768, 128), F32),
-            pltpu.VMEM((4, 768, 128), F32),
             pltpu.SemaphoreType.DMA((KZ,)),
         ],
         compiler_params=grant(40),

time: 91.5 us -> 89 us (0.973)
  Pallas kernels: 18.4 us -> 15.9 us
    pallas_call x1, Pallas kernels: 13.1 us -> 10.6 us  [frequencies(): pl.pallas_call(frequency_kernel, out_shape=jax.ShapeDtypeStruct((16, 4, 1...]
where the time goes in v5:
time: 89 us; the launch traced here: 88.8 us
  blocking collectives  71.9 us (81%)
  Pallas kernels  15.9 us (18%)
  local copies, waits for them, and re-layouts  0.92 us (1%)
    all_to_all x4, blocking collectives, exchange(): return lax.all_to_all(chunks, axes, 0, 0, tiled=True)  71.9 us
    pallas_call x1, Pallas kernels, frequencies(): pl.pallas_call(frequency_kernel, out_shape=jax.ShapeDtypeStruct((16, 4, 1...  10.6 us
    pallas_call x3, Pallas kernels, local_call(): pl.pallas_call(kernel, out_shape=result, in_specs=vmem(len(operands)), ou...  3.97 us

profile of v5, /device:TPU:1, one launch (start us, length us, event | category | flops | bytes accessed | tf_op | source)
XLA Modules:
  0.0 88.8 jit_solution(7947909657071885735)
XLA Ops:
  0.0 0.0 copy-start
  0.0 0.9 %copy-done = bf16[2,76,1,512]{3,0,2,1:T(2,128)(2,1)S(1)} copy-done((bf16[2,76,1,512]{3,0,2,1:T(2,128)(2,1)S(1)}, bf16[2,76,1,512]{3,0,2,1:T(2,128)(2,1)}, u32[]{:S(2)}) %copy-start) | copy-done | bytes 155672
  0.9 0.0 copy-start.1
  0.9 0.6 spread_rows.1
  1.5 23.2 %all_to_all.20.data_ref = bf16[64,16,128]{2,1,0:T(8,128)(2,1)S(1)} all-to-all(bf16[64,16,128]{2,1,0:T(8,128)(2,1)S(1)} %spread_rows.1), channel_id=1, replica_groups=mesh['bx'=32,'by'=2,'col'=2] {'bx','by'}, dimensions={0} | all-to-all | bytes 524288 | tf_op jit(solution)/shard_map/all_to_all | solution.py:369
  24.7 2.0 %to_waves.1 = bf16[64,2,16,128]{3,2,1,0:T(8,128)(2,1)S(1)} custom-call(bf16[64,16,128]{2,1,0:T(8,128)(2,1)S(1)} %all_to_all.20.data_ref), custom_call_target="tpu_custom_call" | custom-call | tf_op jit(solution)/shard_map/to_waves/pallas_call | solution.py:322
  26.7 17.9 %all_to_all.21.spec_ref = bf16[128,16,128]{2,1,0:T(8,128)(2,1)S(1)} all-to-all(bf16[128,16,128]{2,1,0:T(8,128)(2,1)S(1)} %bitcast.9), channel_id=1, replica_groups=mesh['bx'=32,'by'=2,'col'=2] {'bx','by','col'}, dimensions={0} | all-to-all | bytes 1048576 | tf_op jit(solution)/shard_map/all_to_all | solution.py:369
  44.6 10.6 %frequencies.1 = bf16[16,4,16,128]{3,2,1,0:T(8,128)(2,1)S(1)} custom-call(bf16[128,16,128]{2,1,0:T(8,128)(2,1)S(1)} %all_to_all.21.spec_ref, bf16[2,1,17,76,16,152]{5,4,3,2,1,0:T(8,128)(2,1)} %bitcast.14), custom_call_target="tpu_custom_call" | custom-call | tf_op jit(solution)/shard_map/frequencies/pallas_call | solution.py:338
  55.2 15.3 %all_to_all.22.data_ref = bf16[64,16,128]{2,1,0:T(8,128)(2,1)S(1)} all-to-all(bf16[64,16,128]{2,1,0:T(8,128)(2,1)S(1)} %bitcast.10), channel_id=1, replica_groups=mesh['bx'=32,'by'=2,'col'=2] {'bx','by'}, dimensions={0} | all-to-all | bytes 524288 | tf_op jit(solution)/shard_map/all_to_all | solution.py:369
  70.5 1.4 %from_waves.1 = bf16[64,1,16,128]{3,2,1,0:T(8,128)(2,1)S(1)} custom-call(bf16[64,16,128]{2,1,0:T(8,128)(2,1)S(1)} %all_to_all.22.data_ref), custom_call_target="tpu_custom_call" | custom-call | tf_op jit(solution)/shard_map/from_waves/pallas_call | solution.py:322
  71.9 15.6 %all_to_all.23 = bf16[64,16,128]{2,1,0:T(8,128)(2,1)S(1)} all-to-all(bf16[64,16,128]{2,1,0:T(8,128)(2,1)S(1)} %bitcast.11), channel_id=1, replica_groups=mesh['bx'=32,'by'=2,'col'=2] {'bx','by'}, dimensions={0} | all-to-all | bytes 524288 | tf_op jit(solution)/shard_map/all_to_all | solution.py:369
  87.4 0.0 copy-done.1
  87.5 1.3 %from_z.1 = f32[608,128]{1,0:T(8,128)} custom-call(bf16[16,4,16,128]{3,2,1,0:T(8,128)(2,1)S(1)} %bitcast.12, bf16[136,512]{1,0:T(8,128)(2,1)S(1)} %copy-done.1), custom_call_target="tpu_custom_call" | custom-call | tf_op jit(solution)/shard_map/from_z/pallas_call | solution.py:358
Async XLA Ops:
  0.0 0.9 %copy-start = (bf16[2,76,1,512]{3,0,2,1:T(2,128)(2,1)S(1)}, bf16[2,76,1,512]{3,0,2,1:T(2,128)(2,1)}, u32[]{:S(2)}) copy-start(bf16[2,76,1,512]{3,0,2,1:T(2,128)(2,1)} %param.3) | copy-start | bytes 466948
  0.9 86.5 %copy-start.1 = (bf16[136,512]{1,0:T(8,128)(2,1)S(1)}, bf16[136,512]{1,0:T(8,128)(2,1)}, u32[]{:S(2)}) copy-start(bf16[136,512]{1,0:T(8,128)(2,1)} %constant.2.clone.table_ref) | copy-start | bytes 417796

commit v6 on v5

--- a/solution.py
+++ b/solution.py
@@ -172,16 +172,41 @@
     return result
 
 
+def turned(values, steps, sign, lower):
+    if steps == 0:
+        return values
+    cos = math.cos(2 * math.pi * steps / NB)
+    sin = sign * math.sin(2 * math.pi * steps / NB)
+    crossed = pltpu.roll(values, 64, 1) * jnp.where(lower, sin, -sin).astype(F32)
+    return crossed if steps == 8 else values * cos + crossed
+
+
+def short_waves(blocks, sign, lower):
+    count = len(blocks)
+    if count == 1:
+        return blocks
+    even = short_waves(blocks[0::2], sign, lower)
+    odd = short_waves(blocks[1::2], sign, lower)
+    odd = [turned(odd[k], k * (NB // count), sign, lower) for k in range(count // 2)]
+    return [e + o for e, o in zip(even, odd)] + [e - o for e, o in zip(even, odd)]
+
+
 def plane_waves(sign, scale, copies, load, out_ref, middle_ref, end_ref):
     table = line_table()
     for x in range(0, NB, 2):
         pair = [load(i) for i in (x, x + 1)]
         for i, rows in enumerate(line_waves(table, pair, sign)):
             middle_ref[(x + i) * 32 : (x + i + 1) * 32, :] = rows
-    for y in range(0, NB, 2):
-        pair = [middle_ref[pl.ds(i, 32, stride=32), :] for i in (y, y + 1)]
-        for i, rows in enumerate(line_waves(table, pair, sign)):
-            end_ref[pl.ds(y + i, 32, stride=32), :] = rows
+    lower = lane_index(8) < 64
+
+    def column(place, carry):
+        start = pl.multiple_of(place * 8, 8)
+        blocks = [middle_ref[pl.ds(start + x * 32, 8), :] for x in range(NB)]
+        for x, block in enumerate(short_waves(blocks, sign, lower)):
+            end_ref[pl.ds(start + x * 32, 8), :] = block
+        return carry
+
+    lax.fori_loop(0, 4, column, 0)
     total = (end_ref[...] * scale).astype(BF16).reshape(64, 16, 128)
     for copy in range(copies):
         out_ref[:, copy] = total
@@ -190,19 +215,19 @@
 def to_waves_kernel(data_ref, out_ref, start_ref, middle_ref, end_ref):
     high, low = ahead_table()
     data = data_ref[...].reshape(1024, 128)
-    start_ref[...] = dot(data, high) + dot(data, low)
+    start_ref[...] = dot(jnp.concatenate([data, data], 1), jnp.concatenate([high, low], 0))
 
     def load(x):
         return start_ref[x * 32 : x * 32 + 32, :]
 
-    plane_waves(1.0, 1.0 / SCALE**3, 2, load, out_ref, middle_ref, end_ref)
+    plane_waves(1.0, 1.0 / SCALE**2, 2, load, out_ref, middle_ref, end_ref)
 
 
 def from_waves_kernel(data_ref, out_ref, middle_ref, end_ref):
     def load(x):
         return data_ref[2 * x : 2 * x + 2].reshape(32, 128)
 
-    plane_waves(-1.0, 1.0 / (1024 * SCALE**2), 1, load, out_ref, middle_ref, end_ref)
+    plane_waves(-1.0, 1.0 / (1024 * SCALE), 1, load, out_ref, middle_ref, end_ref)
 
 
 def panels(spec_ref, panel_ref, flat_ref, line_ref):
@@ -296,15 +321,21 @@
 
 
 def from_z_kernel(scale, data_ref, table_ref, out_ref):
+    blocks = []
     for group in range(4):
         data = data_ref[:, group].astype(F32)
-        first_row = (group // 2 * 76 + group % 2 * HALF) * 4
         for block in range(2):
             rows = data[:, block * 8 : block * 8 + 8, :].reshape(128, 128)
             last = gather_last(rows[0:8], rows[8:16], 8)
-            full = jnp.concatenate([rows, last], 0).astype(BF16)
-            product = dot_tn(full, table_ref[...])
-            total = (product[0:HALF, :256] + product[64 : 64 + HALF, 256:]) * scale
+            blocks.append(jnp.concatenate([rows, last], 0).astype(BF16))
+    products = dot_tn(jnp.concatenate(blocks, 1), table_ref[...])
+    for group in range(4):
+        first_row = (group // 2 * 76 + group % 2 * HALF) * 4
+        for block in range(2):
+            first = (group * 2 + block) * 128
+            re = products[first : first + HALF, :256]
+            im = products[first + 64 : first + 64 + HALF, 256:]
+            total = (re + im) * scale
             for part in range(2):
                 start = first_row + block * 2 + part
                 out_ref[pl.ds(start, HALF, stride=4), :] = total[:, part * 128 : part * 128 + 128]

time: 89 us -> 89.7 us (level)
  no operation moved by 1% of the time
where the time goes in v6:
time: 89.7 us; the launch traced here: 89.5 us
  blocking collectives  71.9 us (80%)
  Pallas kernels  16.6 us (19%)
  local copies, waits for them, and re-layouts  0.92 us (1%)
    all_to_all x4, blocking collectives, exchange(): return lax.all_to_all(chunks, axes, 0, 0, tiled=True)  71.9 us
    pallas_call x1, Pallas kernels, frequencies(): pl.pallas_call(frequency_kernel, out_shape=jax.ShapeDtypeStruct((16, 4, 1...  10.6 us
    pallas_call x3, Pallas kernels, local_call(): pl.pallas_call(kernel, out_shape=result, in_specs=vmem(len(operands)), ou...  4.61 us

profile of v6, /device:TPU:1, one launch (start us, length us, event | category | flops | bytes accessed | tf_op | source)
XLA Modules:
  0.0 89.5 jit_solution(18275952994710539633)
XLA Ops:
  0.0 0.0 copy-start
  0.0 0.9 %copy-done = bf16[2,76,1,512]{3,0,2,1:T(2,128)(2,1)S(1)} copy-done((bf16[2,76,1,512]{3,0,2,1:T(2,128)(2,1)S(1)}, bf16[2,76,1,512]{3,0,2,1:T(2,128)(2,1)}, u32[]{:S(2)}) %copy-start) | copy-done | bytes 155672
  0.9 0.0 copy-start.1
  0.9 0.6 spread_rows.1
  1.5 23.2 %all_to_all.20.data_ref = bf16[64,16,128]{2,1,0:T(8,128)(2,1)S(1)} all-to-all(bf16[64,16,128]{2,1,0:T(8,128)(2,1)S(1)} %spread_rows.1), channel_id=1, replica_groups=mesh['bx'=32,'by'=2,'col'=2] {'bx','by'}, dimensions={0} | all-to-all | bytes 524288 | tf_op jit(solution)/shard_map/all_to_all | solution.py:400
  24.7 2.3 %to_waves.1 = bf16[64,2,16,128]{3,2,1,0:T(8,128)(2,1)S(1)} custom-call(bf16[64,16,128]{2,1,0:T(8,128)(2,1)S(1)} %all_to_all.20.data_ref), custom_call_target="tpu_custom_call" | custom-call | tf_op jit(solution)/shard_map/to_waves/pallas_call | solution.py:353
  27.0 17.9 %all_to_all.21.spec_ref = bf16[128,16,128]{2,1,0:T(8,128)(2,1)S(1)} all-to-all(bf16[128,16,128]{2,1,0:T(8,128)(2,1)S(1)} %bitcast.9), channel_id=1, replica_groups=mesh['bx'=32,'by'=2,'col'=2] {'bx','by','col'}, dimensions={0} | all-to-all | bytes 1048576 | tf_op jit(solution)/shard_map/all_to_all | solution.py:400
  44.9 10.6 %frequencies.1 = bf16[16,4,16,128]{3,2,1,0:T(8,128)(2,1)S(1)} custom-call(bf16[128,16,128]{2,1,0:T(8,128)(2,1)S(1)} %all_to_all.21.spec_ref, bf16[2,1,17,76,16,152]{5,4,3,2,1,0:T(8,128)(2,1)} %bitcast.14), custom_call_target="tpu_custom_call" | custom-call | tf_op jit(solution)/shard_map/frequencies/pallas_call | solution.py:369
  55.5 15.3 %all_to_all.22.data_ref = bf16[64,16,128]{2,1,0:T(8,128)(2,1)S(1)} all-to-all(bf16[64,16,128]{2,1,0:T(8,128)(2,1)S(1)} %bitcast.10), channel_id=1, replica_groups=mesh['bx'=32,'by'=2,'col'=2] {'bx','by'}, dimensions={0} | all-to-all | bytes 524288 | tf_op jit(solution)/shard_map/all_to_all | solution.py:400
  70.7 1.8 %from_waves.1 = bf16[64,1,16,128]{3,2,1,0:T(8,128)(2,1)S(1)} custom-call(bf16[64,16,128]{2,1,0:T(8,128)(2,1)S(1)} %all_to_all.22.data_ref), custom_call_target="tpu_custom_call" | custom-call | tf_op jit(solution)/shard_map/from_waves/pallas_call | solution.py:353
  72.5 15.6 %all_to_all.23 = bf16[64,16,128]{2,1,0:T(8,128)(2,1)S(1)} all-to-all(bf16[64,16,128]{2,1,0:T(8,128)(2,1)S(1)} %bitcast.11), channel_id=1, replica_groups=mesh['bx'=32,'by'=2,'col'=2] {'bx','by'}, dimensions={0} | all-to-all | bytes 524288 | tf_op jit(solution)/shard_map/all_to_all | solution.py:400
  88.1 0.0 copy-done.1
  88.1 1.4 %from_z.1 = f32[608,128]{1,0:T(8,128)} custom-call(bf16[16,4,16,128]{3,2,1,0:T(8,128)(2,1)S(1)} %bitcast.12, bf16[136,512]{1,0:T(8,128)(2,1)S(1)} %copy-done.1), custom_call_target="tpu_custom_call" | custom-call | tf_op jit(solution)/shard_map/from_z/pallas_call | solution.py:389
Async XLA Ops:
  0.0 0.9 %copy-start = (bf16[2,76,1,512]{3,0,2,1:T(2,128)(2,1)S(1)}, bf16[2,76,1,512]{3,0,2,1:T(2,128)(2,1)}, u32[]{:S(2)}) copy-start(bf16[2,76,1,512]{3,0,2,1:T(2,128)(2,1)} %param.3) | copy-start | bytes 466948
  0.9 87.2 %copy-start.1 = (bf16[136,512]{1,0:T(8,128)(2,1)S(1)}, bf16[136,512]{1,0:T(8,128)(2,1)}, u32[]{:S(2)}) copy-start(bf16[136,512]{1,0:T(8,128)(2,1)} %constant.2.clone.table_ref) | copy-start | bytes 417796

commit v7 on v6

--- a/solution.py
+++ b/solution.py
@@ -139,7 +139,6 @@
         for rhs in range(RHS):
             part = field[:, rhs, tile * 128 : tile * 128 + 128]
             rows_ref[tile, rhs * 76 : rhs * 76 + 76, :] = part
-    chunk_ref[896:1024, :] = jnp.zeros((128, 128), F32)
     slot = lane_index(56) // NB
     for tile in range(4):
         parts = [rows_ref[tile, pl.ds(row, 56, stride=ROWS), :] for row in range(ROWS)]
@@ -149,8 +148,10 @@
                 shift = (row - y) % 4 * NB
                 moved = pltpu.roll(parts[row], shift, 1) if shift else parts[row]
                 total = jnp.where(slot == row, moved, total)
-            chunk_ref[pl.ds(tile * 4 + y, 56, stride=16), :] = total
-    out_ref[...] = chunk_ref[...].astype(BF16).reshape(64, 16, 128)
+            chunk_ref[pl.ds(tile * 4 + y, 56, stride=24), :] = total
+    for owner in range(56):
+        out_ref[owner] = chunk_ref[owner * 24 : owner * 24 + 16, :].astype(BF16)
+    out_ref[56:64] = jnp.zeros((8, 16, 128), BF16)
 
 
 def line_waves(table, pair, sign):
@@ -200,13 +201,14 @@
     lower = lane_index(8) < 64
 
     def column(place, carry):
-        start = pl.multiple_of(place * 8, 8)
+        start = place * 8
         blocks = [middle_ref[pl.ds(start + x * 32, 8), :] for x in range(NB)]
         for x, block in enumerate(short_waves(blocks, sign, lower)):
             end_ref[pl.ds(start + x * 32, 8), :] = block
         return carry
 
-    lax.fori_loop(0, 4, column, 0)
+    for place in range(4):
+        column(place, 0)
     total = (end_ref[...] * scale).astype(BF16).reshape(64, 16, 128)
     for copy in range(copies):
         out_ref[:, copy] = total
@@ -231,18 +233,22 @@
 
 
 def panels(spec_ref, panel_ref, flat_ref, line_ref):
-    flat_ref[...] = spec_ref[...].astype(F32).reshape(2048, 128)
+    for source in range(128):
+        flat_ref[source * 24 : source * 24 + 16, :] = spec_ref[source].astype(F32)
     pick = pick_table()
     for ky in range(0, 16, 2):
-        both = [flat_ref[pl.ds(i, 128, stride=16), :] for i in (ky, ky + 1)]
+        both = [flat_ref[pl.ds(i, 128, stride=24), :] for i in (ky, ky + 1)]
         turned = dot_nt(pick, jnp.concatenate(both, 0).astype(BF16))
         for i in range(2):
             for row in range(ROWS):
                 for part in range(2):
                     block = turned[(row * 2 + part) * 24 : (row * 2 + part) * 24 + 24]
-                    place = pl.ds(part * 16 + ky + i, 24, stride=32)
+                    place = pl.ds(part * 16 + ky + i, 24, stride=40)
                     line_ref[row, place, :] = block[:, i * 128 : i * 128 + 128]
-    lines = [line_ref[row, 0 : KZ * 32, :].astype(BF16) for row in range(ROWS)]
+    lines = []
+    for row in range(ROWS):
+        blocks = [line_ref[row, kz * 40 : kz * 40 + 32, :].astype(BF16) for kz in range(KZ)]
+        lines.append(jnp.concatenate(blocks, 0))
     total = dot(jnp.concatenate(lines, 1), select_in()).astype(BF16)
     for kz in range(KZ):
         re = total[kz * 32 : kz * 32 + 16]
@@ -376,8 +382,8 @@
             pltpu.VMEM((KZ, 2, 76, 16, 152), BF16),
             pltpu.VMEM((KZ, 64, 512), BF16),
             pltpu.VMEM((KZ, 64, 1216), BF16),
-            pltpu.VMEM((2048, 128), F32),
-            pltpu.VMEM((ROWS, 768, 128), F32),
+            pltpu.VMEM((3072, 128), F32),
+            pltpu.VMEM((ROWS, 960, 128), F32),
             pltpu.SemaphoreType.DMA((KZ,)),
         ],
         compiler_params=grant(40),
@@ -405,7 +411,7 @@
     plane = (1024, 128)
     field = multipoles[:, :, 0, :].transpose(1, 0, 2)
     rows = local_call(
-        spread_rows_kernel, "spread_rows", chunks_of(64, 16, 128), [(4, 168, 128), plane], field
+        spread_rows_kernel, "spread_rows", chunks_of(64, 16, 128), [(4, 168, 128), (1344, 128)], field
     )
     rows = exchange(rows, near)
     spectrum = local_call(

time: 89.7 us -> 87.5 us (0.975)
  Pallas kernels: 16.6 us -> 14.4 us
    pallas_call x3, Pallas kernels: 4.61 us -> 2.66 us  [local_call(): pl.pallas_call(kernel, out_shape=result, in_specs=vmem(len(operands)), ou...]
where the time goes in v7:
time: 87.5 us; the launch traced here: 87.3 us
  blocking collectives  71.9 us (82%)
  Pallas kernels  14.4 us (16%)
  local copies, waits for them, and re-layouts  0.92 us (1%)
    all_to_all x4, blocking collectives, exchange(): return lax.all_to_all(chunks, axes, 0, 0, tiled=True)  71.9 us
    pallas_call x1, Pallas kernels, frequencies(): pl.pallas_call(frequency_kernel, out_shape=jax.ShapeDtypeStruct((16, 4, 1...  10.4 us
    pallas_call x3, Pallas kernels, local_call(): pl.pallas_call(kernel, out_shape=result, in_specs=vmem(len(operands)), ou...  2.66 us

profile of v7, /device:TPU:1, one launch (start us, length us, event | category | flops | bytes accessed | tf_op | source)
XLA Modules:
  0.0 87.3 jit_solution(7568955294197901218)
XLA Ops:
  0.0 0.0 copy-start
  0.0 0.9 %copy-done = bf16[2,76,1,512]{3,0,2,1:T(2,128)(2,1)S(1)} copy-done((bf16[2,76,1,512]{3,0,2,1:T(2,128)(2,1)S(1)}, bf16[2,76,1,512]{3,0,2,1:T(2,128)(2,1)}, u32[]{:S(2)}) %copy-start) | copy-done | bytes 155672
  0.9 0.0 copy-start.1
  0.9 0.5 spread_rows.1
  1.4 23.2 %all_to_all.20.data_ref = bf16[64,16,128]{2,1,0:T(8,128)(2,1)S(1)} all-to-all(bf16[64,16,128]{2,1,0:T(8,128)(2,1)S(1)} %spread_rows.1), channel_id=1, replica_groups=mesh['bx'=32,'by'=2,'col'=2] {'bx','by'}, dimensions={0} | all-to-all | bytes 524288 | tf_op jit(solution)/shard_map/all_to_all | solution.py:406
  24.7 1.3 %to_waves.1 = bf16[64,2,16,128]{3,2,1,0:T(8,128)(2,1)S(1)} custom-call(bf16[64,16,128]{2,1,0:T(8,128)(2,1)S(1)} %all_to_all.20.data_ref), custom_call_target="tpu_custom_call" | custom-call | tf_op jit(solution)/shard_map/to_waves/pallas_call | solution.py:359
  26.0 17.9 %all_to_all.21.spec_ref = bf16[128,16,128]{2,1,0:T(8,128)(2,1)S(1)} all-to-all(bf16[128,16,128]{2,1,0:T(8,128)(2,1)S(1)} %bitcast.9), channel_id=1, replica_groups=mesh['bx'=32,'by'=2,'col'=2] {'bx','by','col'}, dimensions={0} | all-to-all | bytes 1048576 | tf_op jit(solution)/shard_map/all_to_all | solution.py:406
  43.9 10.4 %frequencies.1 = bf16[16,4,16,128]{3,2,1,0:T(8,128)(2,1)S(1)} custom-call(bf16[128,16,128]{2,1,0:T(8,128)(2,1)S(1)} %all_to_all.21.spec_ref, bf16[2,1,17,76,16,152]{5,4,3,2,1,0:T(8,128)(2,1)} %bitcast.14), custom_call_target="tpu_custom_call" | custom-call | tf_op jit(solution)/shard_map/frequencies/pallas_call | solution.py:375
  54.2 15.3 %all_to_all.22.data_ref = bf16[64,16,128]{2,1,0:T(8,128)(2,1)S(1)} all-to-all(bf16[64,16,128]{2,1,0:T(8,128)(2,1)S(1)} %bitcast.10), channel_id=1, replica_groups=mesh['bx'=32,'by'=2,'col'=2] {'bx','by'}, dimensions={0} | all-to-all | bytes 524288 | tf_op jit(solution)/shard_map/all_to_all | solution.py:406
  69.5 0.8 from_waves.1
  70.4 15.6 %all_to_all.23 = bf16[64,16,128]{2,1,0:T(8,128)(2,1)S(1)} all-to-all(bf16[64,16,128]{2,1,0:T(8,128)(2,1)S(1)} %bitcast.11), channel_id=1, replica_groups=mesh['bx'=32,'by'=2,'col'=2] {'bx','by'}, dimensions={0} | all-to-all | bytes 524288 | tf_op jit(solution)/shard_map/all_to_all | solution.py:406
  85.9 0.0 copy-done.1
  85.9 1.4 %from_z.1 = f32[608,128]{1,0:T(8,128)} custom-call(bf16[16,4,16,128]{3,2,1,0:T(8,128)(2,1)S(1)} %bitcast.12, bf16[136,512]{1,0:T(8,128)(2,1)S(1)} %copy-done.1), custom_call_target="tpu_custom_call" | custom-call | tf_op jit(solution)/shard_map/from_z/pallas_call | solution.py:395
Async XLA Ops:
  0.0 0.9 %copy-start = (bf16[2,76,1,512]{3,0,2,1:T(2,128)(2,1)S(1)}, bf16[2,76,1,512]{3,0,2,1:T(2,128)(2,1)}, u32[]{:S(2)}) copy-start(bf16[2,76,1,512]{3,0,2,1:T(2,128)(2,1)} %param.3) | copy-start | bytes 466948
  0.9 85.0 %copy-start.1 = (bf16[136,512]{1,0:T(8,128)(2,1)S(1)}, bf16[136,512]{1,0:T(8,128)(2,1)}, u32[]{:S(2)}) copy-start(bf16[136,512]{1,0:T(8,128)(2,1)} %constant.2.clone.table_ref) | copy-start | bytes 417796

commit v8 on v7

--- a/solution.py
+++ b/solution.py
@@ -15,6 +15,7 @@
 HALF = 38
 SPARE = 19
 ROWS = 3
+HEAD = 3
 F32 = jnp.float32
 BF16 = jnp.bfloat16
 
@@ -214,7 +215,16 @@
         out_ref[:, copy] = total
 
 
-def to_waves_kernel(data_ref, out_ref, start_ref, middle_ref, end_ref):
+def kernel_copy(kernel_hbm, target_ref, sem, kz, place):
+    return pltpu.make_async_copy(kernel_hbm.at[:, 0, kz], target_ref.at[place], sem.at[place])
+
+
+def to_waves_kernel(
+    data_ref, kernel_hbm, out_ref, head_ref, start_ref, middle_ref, end_ref, head_sem
+):
+    copies = [kernel_copy(kernel_hbm, head_ref, head_sem, kz, kz) for kz in range(HEAD)]
+    for copy in copies:
+        copy.start()
     high, low = ahead_table()
     data = data_ref[...].reshape(1024, 128)
     start_ref[...] = dot(jnp.concatenate([data, data], 1), jnp.concatenate([high, low], 0))
@@ -223,6 +233,8 @@
         return start_ref[x * 32 : x * 32 + 32, :]
 
     plane_waves(1.0, 1.0 / SCALE**2, 2, load, out_ref, middle_ref, end_ref)
+    for copy in copies:
+        copy.wait()
 
 
 def from_waves_kernel(data_ref, out_ref, middle_ref, end_ref):
@@ -265,6 +277,7 @@
 
 def frequency_kernel(
     spec_ref,
+    head_ref,
     kernel_hbm,
     out_ref,
     back_ref,
@@ -276,11 +289,9 @@
     kernel_sem,
 ):
     def load(kz):
-        return pltpu.make_async_copy(
-            kernel_hbm.at[:, 0, kz], kernel_ref.at[kz], kernel_sem.at[kz]
-        )
-
-    for kz in range(KZ):
+        return kernel_copy(kernel_hbm, kernel_ref, kernel_sem, kz, kz - HEAD)
+
+    for kz in range(HEAD, KZ):
         load(kz).start()
     panels(spec_ref, panel_ref, flat_ref, line_ref)
     back_ref[...] = select_out()
@@ -289,25 +300,29 @@
     lane = lax.broadcasted_iota(jnp.int32, (64, 128), 1)
     same = row % 16 == lane % 16
 
-    def step(kz):
+    def step(kz, matrix_ref, place):
         panel = panel_ref[kz]
-        product = dot_nt(panel[:, 0:152], kernel_ref[kz, 0].reshape(1216, 152))
-        product += dot_nt(panel[:, 256:408], kernel_ref[kz, 1].reshape(1216, 152))
+        product = dot_nt(panel[:, 0:152], matrix_ref[place, 0].reshape(1216, 152))
+        product += dot_nt(panel[:, 256:408], matrix_ref[place, 1].reshape(1216, 152))
         for tile in range(0, 1216, 128):
             wide = min(128, 1216 - tile)
             part = jnp.where(same[:, :wide], product[:, tile : tile + wide], 0.0)
             own_ref[kz, :, tile : tile + wide] = part.astype(BF16)
 
+    def ahead(kz, carry):
+        step(kz, head_ref, kz)
+        return carry
+
     def pair(half, carry):
-        for kz in (2 * half, 2 * half + 1):
-            load(kz).wait()
-        for kz in (2 * half, 2 * half + 1):
-            step(kz)
+        places = (2 * half, 2 * half + 1)
+        for place in places:
+            load(place + HEAD).wait()
+        for place in places:
+            step(place + HEAD, kernel_ref, place)
         return carry
 
-    lax.fori_loop(0, KZ // 2, pair, 0)
-    load(KZ - 1).wait()
-    step(KZ - 1)
+    lax.fori_loop(0, HEAD, ahead, 0)
+    lax.fori_loop(0, (KZ - HEAD) // 2, pair, 0)
 
     local = dot(own_ref[...].reshape(KZ * 64, 1216), back_ref[...]).reshape(KZ, 64, 256)
     for kz in range(KZ):
@@ -326,25 +341,29 @@
                     out_ref[block, group] = whole.astype(BF16)
 
 
-def from_z_kernel(scale, data_ref, table_ref, out_ref):
-    blocks = []
+def from_z_kernel(scale, data_ref, table_ref, out_hbm, out_ref, sem):
+    copies = []
     for group in range(4):
         data = data_ref[:, group].astype(F32)
+        blocks = []
         for block in range(2):
             rows = data[:, block * 8 : block * 8 + 8, :].reshape(128, 128)
             last = gather_last(rows[0:8], rows[8:16], 8)
             blocks.append(jnp.concatenate([rows, last], 0).astype(BF16))
-    products = dot_tn(jnp.concatenate(blocks, 1), table_ref[...])
-    for group in range(4):
-        first_row = (group // 2 * 76 + group % 2 * HALF) * 4
+        products = dot_tn(jnp.concatenate(blocks, 1), table_ref[...])
+        first_row = group * HALF * 4
         for block in range(2):
-            first = (group * 2 + block) * 128
-            re = products[first : first + HALF, :256]
-            im = products[first + 64 : first + 64 + HALF, 256:]
+            re = products[block * 128 : block * 128 + HALF, :256]
+            im = products[block * 128 + 64 : block * 128 + 64 + HALF, 256:]
             total = (re + im) * scale
             for part in range(2):
                 start = first_row + block * 2 + part
                 out_ref[pl.ds(start, HALF, stride=4), :] = total[:, part * 128 : part * 128 + 128]
+        rows = pl.ds(first_row, HALF * 4)
+        copies.append(pltpu.make_async_copy(out_ref.at[rows], out_hbm.at[rows], sem.at[group]))
+        copies[-1].start()
+    for copy in copies:
+        copy.wait()
 
 
 def vmem(count):
@@ -371,24 +390,37 @@
     return jax.ShapeDtypeStruct(shape, BF16)
 
 
-def frequencies(spectrum, kernel):
+def to_waves(rows, kernel):
+    plane = pltpu.VMEM((1024, 128), F32)
+    return pl.pallas_call(
+        to_waves_kernel,
+        out_shape=(chunks_of(64, 2, 16, 128), chunks_of(HEAD, 2, 76, 16, 152)),
+        in_specs=vmem(1) + [pl.BlockSpec(memory_space=pltpu.HBM)],
+        out_specs=tuple(vmem(2)),
+        scratch_shapes=[plane, plane, plane, pltpu.SemaphoreType.DMA((HEAD,))],
+        compiler_params=grant(40),
+        name="to_waves",
+    )(rows, kernel)
+
+
+def frequencies(spectrum, head, kernel):
     return pl.pallas_call(
         frequency_kernel,
         out_shape=jax.ShapeDtypeStruct((16, 4, 16, 128), BF16),
-        in_specs=vmem(1) + [pl.BlockSpec(memory_space=pltpu.HBM)],
+        in_specs=vmem(2) + [pl.BlockSpec(memory_space=pltpu.HBM)],
         out_specs=pl.BlockSpec(memory_space=pltpu.VMEM),
         scratch_shapes=[
             pltpu.VMEM((1216, 256), BF16),
-            pltpu.VMEM((KZ, 2, 76, 16, 152), BF16),
+            pltpu.VMEM((KZ - HEAD, 2, 76, 16, 152), BF16),
             pltpu.VMEM((KZ, 64, 512), BF16),
             pltpu.VMEM((KZ, 64, 1216), BF16),
             pltpu.VMEM((3072, 128), F32),
             pltpu.VMEM((ROWS, 960, 128), F32),
-            pltpu.SemaphoreType.DMA((KZ,)),
+            pltpu.SemaphoreType.DMA((KZ - HEAD,)),
         ],
         compiler_params=grant(40),
         name="frequencies",
-    )(spectrum, kernel)
+    )(spectrum, head, kernel)
 
 
 def from_z(data, table, scale):
@@ -396,7 +428,8 @@
         functools.partial(from_z_kernel, scale),
         out_shape=jax.ShapeDtypeStruct((608, 128), F32),
         in_specs=vmem(2),
-        out_specs=pl.BlockSpec(memory_space=pltpu.VMEM),
+        out_specs=pl.BlockSpec(memory_space=pltpu.HBM),
+        scratch_shapes=[pltpu.VMEM((608, 128), F32), pltpu.SemaphoreType.DMA((4,))],
         compiler_params=grant(8),
         name="from_z",
     )(data, table)
@@ -414,11 +447,10 @@
         spread_rows_kernel, "spread_rows", chunks_of(64, 16, 128), [(4, 168, 128), (1344, 128)], field
     )
     rows = exchange(rows, near)
-    spectrum = local_call(
-        to_waves_kernel, "to_waves", chunks_of(64, 2, 16, 128), [plane, plane, plane], rows
-    )
+    kernel = kernel.transpose(0, 1, 3, 4, 2, 5)
+    spectrum, head = to_waves(rows, kernel)
     spectrum = exchange(spectrum.reshape(128, 16, 128), ("bx", "by", "col"))
-    local = frequencies(spectrum, kernel.transpose(0, 1, 3, 4, 2, 5))
+    local = frequencies(spectrum, head, kernel)
     local = exchange(local.reshape(64, 16, 128), near)
     back = local_call(
         from_waves_kernel, "from_waves", chunks_of(64, 1, 16, 128), [plane, plane], local

time: 87.5 us -> 88.9 us (1.016)
  Pallas kernels: 14.4 us -> 15.8 us
    pallas_call x0 -> x1, Pallas kernels: none -> 3.3 us  [to_waves(): pl.pallas_call(to_waves_kernel, out_shape=(chunks_of(64, 2, 16, 128), chu...]
    pallas_call x3 -> x2, Pallas kernels: 2.66 us -> 1.35 us  [local_call(): pl.pallas_call(kernel, out_shape=result, in_specs=vmem(len(operands)), ou...]
where the time goes in v8:
time: 88.9 us; the launch traced here: 88.6 us
  blocking collectives  71.9 us (81%)
  Pallas kernels  15.8 us (18%)
  local copies, waits for them, and re-layouts  0.92 us (1%)
    all_to_all x4, blocking collectives, exchange(): return lax.all_to_all(chunks, axes, 0, 0, tiled=True)  71.9 us
    pallas_call x1, Pallas kernels, frequencies(): pl.pallas_call(frequency_kernel, out_shape=jax.ShapeDtypeStruct((16, 4, 1...  9.87 us
    pallas_call x1, Pallas kernels, to_waves(): pl.pallas_call(to_waves_kernel, out_shape=(chunks_of(64, 2, 16, 128), chu...  3.3 us

profile of v8, /device:TPU:1, one launch (start us, length us, event | category | flops | bytes accessed | tf_op | source)
XLA Modules:
  0.0 88.6 jit_solution(3314159667322596675)
XLA Ops:
  0.0 0.0 copy-start
  0.0 0.9 %copy-done = bf16[2,76,1,512]{3,0,2,1:T(2,128)(2,1)S(1)} copy-done((bf16[2,76,1,512]{3,0,2,1:T(2,128)(2,1)S(1)}, bf16[2,76,1,512]{3,0,2,1:T(2,128)(2,1)}, u32[]{:S(2)}) %copy-start) | copy-done | bytes 155672
  0.9 0.5 spread_rows.1
  1.4 23.2 %all_to_all.20.data_ref = bf16[64,16,128]{2,1,0:T(8,128)(2,1)S(1)} all-to-all(bf16[64,16,128]{2,1,0:T(8,128)(2,1)S(1)} %spread_rows.1), channel_id=1, replica_groups=mesh['bx'=32,'by'=2,'col'=2] {'bx','by'}, dimensions={0} | all-to-all | bytes 524288 | tf_op jit(solution)/shard_map/all_to_all | solution.py:439
  24.7 0.0 copy-start.1
  24.7 3.3 %to_waves.1 = (bf16[64,2,16,128]{3,2,1,0:T(8,128)(2,1)S(1)}, bf16[3,2,76,16,152]{4,3,2,1,0:T(8,128)(2,1)S(1)}) custom-call(bf16[64,16,128]{2,1,0:T(8,128)(2,1)S(1)} %all_to_all.20.data_ref, bf16[2,1,17,76,16,152]{5,4,3,2,1,0:T(8,128)(2,1)} %bitcast.14), custom_call_target="tpu_custom_call" | custom-call | tf_op jit(solution)/shard_map/to_waves/pallas_call | solution.py:395
  28.0 17.9 %all_to_all.21.spec_ref = bf16[128,16,128]{2,1,0:T(8,128)(2,1)S(1)} all-to-all(bf16[128,16,128]{2,1,0:T(8,128)(2,1)S(1)} %bitcast.12), channel_id=1, replica_groups=mesh['bx'=32,'by'=2,'col'=2] {'bx','by','col'}, dimensions={0} | all-to-all | bytes 1048576 | tf_op jit(solution)/shard_map/all_to_all | solution.py:439
  45.9 9.9 %frequencies.1 = bf16[16,4,16,128]{3,2,1,0:T(8,128)(2,1)S(1)} custom-call(bf16[128,16,128]{2,1,0:T(8,128)(2,1)S(1)} %all_to_all.21.spec_ref, bf16[3,2,76,16,152]{4,3,2,1,0:T(8,128)(2,1)S(1)} %get-tuple-element.8.head_ref, bf16[2,1,17,76,16,152]{5,4,3,2,1,0:T(8,128)(2,1)} %bitcast.15), custom_call_target="tpu_custom_call" | custom-call | tf_op jit(solution)/shard_map/frequencies/pallas_call | solution.py:407
  55.7 15.3 %all_to_all.22.data_ref = bf16[64,16,128]{2,1,0:T(8,128)(2,1)S(1)} all-to-all(bf16[64,16,128]{2,1,0:T(8,128)(2,1)S(1)} %bitcast.9), channel_id=1, replica_groups=mesh['bx'=32,'by'=2,'col'=2] {'bx','by'}, dimensions={0} | all-to-all | bytes 524288 | tf_op jit(solution)/shard_map/all_to_all | solution.py:439
  71.0 0.8 from_waves.1
  71.8 15.6 %all_to_all.23 = bf16[64,16,128]{2,1,0:T(8,128)(2,1)S(1)} all-to-all(bf16[64,16,128]{2,1,0:T(8,128)(2,1)S(1)} %bitcast.10), channel_id=1, replica_groups=mesh['bx'=32,'by'=2,'col'=2] {'bx','by'}, dimensions={0} | all-to-all | bytes 524288 | tf_op jit(solution)/shard_map/all_to_all | solution.py:439
  87.4 0.0 copy-done.1
  87.4 1.2 %from_z.1 = f32[608,128]{1,0:T(8,128)} custom-call(bf16[16,4,16,128]{3,2,1,0:T(8,128)(2,1)S(1)} %bitcast.11, bf16[136,512]{1,0:T(8,128)(2,1)S(1)} %copy-done.1), custom_call_target="tpu_custom_call" | custom-call | tf_op jit(solution)/shard_map/from_z/pallas_call | solution.py:427
Async XLA Ops:
  0.0 0.9 %copy-start = (bf16[2,76,1,512]{3,0,2,1:T(2,128)(2,1)S(1)}, bf16[2,76,1,512]{3,0,2,1:T(2,128)(2,1)}, u32[]{:S(2)}) copy-start(bf16[2,76,1,512]{3,0,2,1:T(2,128)(2,1)} %param.3) | copy-start | bytes 466948
  24.7 62.7 %copy-start.1 = (bf16[136,512]{1,0:T(8,128)(2,1)S(1)}, bf16[136,512]{1,0:T(8,128)(2,1)}, u32[]{:S(2)}) copy-start(bf16[136,512]{1,0:T(8,128)(2,1)} %constant.2.clone.table_ref) | copy-start | bytes 417796

commit v9 on v7

--- a/solution.py
+++ b/solution.py
@@ -326,25 +326,29 @@
                     out_ref[block, group] = whole.astype(BF16)
 
 
-def from_z_kernel(scale, data_ref, table_ref, out_ref):
-    blocks = []
+def from_z_kernel(scale, data_ref, table_ref, out_hbm, out_ref, sem):
+    copies = []
     for group in range(4):
         data = data_ref[:, group].astype(F32)
+        blocks = []
         for block in range(2):
             rows = data[:, block * 8 : block * 8 + 8, :].reshape(128, 128)
             last = gather_last(rows[0:8], rows[8:16], 8)
             blocks.append(jnp.concatenate([rows, last], 0).astype(BF16))
-    products = dot_tn(jnp.concatenate(blocks, 1), table_ref[...])
-    for group in range(4):
-        first_row = (group // 2 * 76 + group % 2 * HALF) * 4
+        products = dot_tn(jnp.concatenate(blocks, 1), table_ref[...])
+        first_row = group * HALF * 4
         for block in range(2):
-            first = (group * 2 + block) * 128
-            re = products[first : first + HALF, :256]
-            im = products[first + 64 : first + 64 + HALF, 256:]
+            re = products[block * 128 : block * 128 + HALF, :256]
+            im = products[block * 128 + 64 : block * 128 + 64 + HALF, 256:]
             total = (re + im) * scale
             for part in range(2):
                 start = first_row + block * 2 + part
                 out_ref[pl.ds(start, HALF, stride=4), :] = total[:, part * 128 : part * 128 + 128]
+        rows = pl.ds(first_row, HALF * 4)
+        copies.append(pltpu.make_async_copy(out_ref.at[rows], out_hbm.at[rows], sem.at[group]))
+        copies[-1].start()
+    for copy in copies:
+        copy.wait()
 
 
 def vmem(count):
@@ -396,7 +400,8 @@
         functools.partial(from_z_kernel, scale),
         out_shape=jax.ShapeDtypeStruct((608, 128), F32),
         in_specs=vmem(2),
-        out_specs=pl.BlockSpec(memory_space=pltpu.VMEM),
+        out_specs=pl.BlockSpec(memory_space=pltpu.HBM),
+        scratch_shapes=[pltpu.VMEM((608, 128), F32), pltpu.SemaphoreType.DMA((4,))],
         compiler_params=grant(8),
         name="from_z",
     )(data, table)

time: 87.5 us -> 87.4 us (level)
  no operation moved by 1% of the time
where the time goes in v9:
time: 87.4 us; the launch traced here: 87.2 us
  blocking collectives  71.9 us (82%)
  Pallas kernels  14.3 us (16%)
  local copies, waits for them, and re-layouts  0.92 us (1%)
    all_to_all x4, blocking collectives, exchange(): return lax.all_to_all(chunks, axes, 0, 0, tiled=True)  71.9 us
    pallas_call x1, Pallas kernels, frequencies(): pl.pallas_call(frequency_kernel, out_shape=jax.ShapeDtypeStruct((16, 4, 1...  10.4 us
    pallas_call x3, Pallas kernels, local_call(): pl.pallas_call(kernel, out_shape=result, in_specs=vmem(len(operands)), ou...  2.66 us

profile of v9, /device:TPU:1, one launch (start us, length us, event | category | flops | bytes accessed | tf_op | source)
XLA Modules:
  0.0 87.2 jit_solution(1880981015039042508)
XLA Ops:
  0.0 0.0 copy-start
  0.0 0.9 %copy-done = bf16[2,76,1,512]{3,0,2,1:T(2,128)(2,1)S(1)} copy-done((bf16[2,76,1,512]{3,0,2,1:T(2,128)(2,1)S(1)}, bf16[2,76,1,512]{3,0,2,1:T(2,128)(2,1)}, u32[]{:S(2)}) %copy-start) | copy-done | bytes 155672
  0.9 0.0 copy-start.1
  0.9 0.5 spread_rows.1
  1.4 23.2 %all_to_all.20.data_ref = bf16[64,16,128]{2,1,0:T(8,128)(2,1)S(1)} all-to-all(bf16[64,16,128]{2,1,0:T(8,128)(2,1)S(1)} %spread_rows.1), channel_id=1, replica_groups=mesh['bx'=32,'by'=2,'col'=2] {'bx','by'}, dimensions={0} | all-to-all | bytes 524288 | tf_op jit(solution)/shard_map/all_to_all | solution.py:411
  24.7 1.3 %to_waves.1 = bf16[64,2,16,128]{3,2,1,0:T(8,128)(2,1)S(1)} custom-call(bf16[64,16,128]{2,1,0:T(8,128)(2,1)S(1)} %all_to_all.20.data_ref), custom_call_target="tpu_custom_call" | custom-call | tf_op jit(solution)/shard_map/to_waves/pallas_call | solution.py:363
  26.0 17.9 %all_to_all.21.spec_ref = bf16[128,16,128]{2,1,0:T(8,128)(2,1)S(1)} all-to-all(bf16[128,16,128]{2,1,0:T(8,128)(2,1)S(1)} %bitcast.9), channel_id=1, replica_groups=mesh['bx'=32,'by'=2,'col'=2] {'bx','by','col'}, dimensions={0} | all-to-all | bytes 1048576 | tf_op jit(solution)/shard_map/all_to_all | solution.py:411
  43.9 10.4 %frequencies.1 = bf16[16,4,16,128]{3,2,1,0:T(8,128)(2,1)S(1)} custom-call(bf16[128,16,128]{2,1,0:T(8,128)(2,1)S(1)} %all_to_all.21.spec_ref, bf16[2,1,17,76,16,152]{5,4,3,2,1,0:T(8,128)(2,1)} %bitcast.14), custom_call_target="tpu_custom_call" | custom-call | tf_op jit(solution)/shard_map/frequencies/pallas_call | solution.py:379
  54.2 15.3 %all_to_all.22.data_ref = bf16[64,16,128]{2,1,0:T(8,128)(2,1)S(1)} all-to-all(bf16[64,16,128]{2,1,0:T(8,128)(2,1)S(1)} %bitcast.10), channel_id=1, replica_groups=mesh['bx'=32,'by'=2,'col'=2] {'bx','by'}, dimensions={0} | all-to-all | bytes 524288 | tf_op jit(solution)/shard_map/all_to_all | solution.py:411
  69.5 0.8 from_waves.1
  70.4 15.6 %all_to_all.23 = bf16[64,16,128]{2,1,0:T(8,128)(2,1)S(1)} all-to-all(bf16[64,16,128]{2,1,0:T(8,128)(2,1)S(1)} %bitcast.11), channel_id=1, replica_groups=mesh['bx'=32,'by'=2,'col'=2] {'bx','by'}, dimensions={0} | all-to-all | bytes 524288 | tf_op jit(solution)/shard_map/all_to_all | solution.py:411
  85.9 0.0 copy-done.1
  85.9 1.2 %from_z.1 = f32[608,128]{1,0:T(8,128)} custom-call(bf16[16,4,16,128]{3,2,1,0:T(8,128)(2,1)S(1)} %bitcast.12, bf16[136,512]{1,0:T(8,128)(2,1)S(1)} %copy-done.1), custom_call_target="tpu_custom_call" | custom-call | tf_op jit(solution)/shard_map/from_z/pallas_call | solution.py:399
Async XLA Ops:
  0.0 0.9 %copy-start = (bf16[2,76,1,512]{3,0,2,1:T(2,128)(2,1)S(1)}, bf16[2,76,1,512]{3,0,2,1:T(2,128)(2,1)}, u32[]{:S(2)}) copy-start(bf16[2,76,1,512]{3,0,2,1:T(2,128)(2,1)} %param.3) | copy-start | bytes 466948
  0.9 85.0 %copy-start.1 = (bf16[136,512]{1,0:T(8,128)(2,1)S(1)}, bf16[136,512]{1,0:T(8,128)(2,1)}, u32[]{:S(2)}) copy-start(bf16[136,512]{1,0:T(8,128)(2,1)} %constant.2.clone.table_ref) | copy-start | bytes 417796
